TPU v7x, 32 devices: a whole 2x2x4 slice. The times are simulated.
32 devices in a mesh: dp: 16 (over z, y, core), tensor: 2 (over x).
Axes of the slice: x: 2, y: 2, z: 4, core: 2. Of those that a mesh axis runs over, the one named last changes fastest.
Arguments:
- tokens: bfloat16 [8192, 1024], P('dp'), may hold values from -6 to 6
- clip_lengths: int32 [16, 3], P('dp'), may hold values from 0 to 512, as said below
- attn_gain: float32 [1024], replicated, may hold values from 0.5 to 1.5
- attn_shift: float32 [1024], replicated, may hold values from -3 to 3
- qkv_weight: bfloat16 [3, 1024, 1024], P(None, None, 'tensor'), may hold values from -0.1875 to 0.1875
- qv_bias: float32 [2, 1024], P(None, 'tensor'), may hold values from -0.3 to 0.3
- out_weight: bfloat16 [1024, 1024], P('tensor'), may hold values from -4 to 4
- out_bias: float32 [1024], replicated, may hold values from -3 to 3
- mlp_gain: float32 [1024], replicated, may hold values from 0.5 to 1.5
- mlp_shift: float32 [1024], replicated, may hold values from -3 to 3
- up_weight: bfloat16 [1024, 4096], P(None, 'tensor'), may hold values from -0.1875 to 0.1875
- up_bias: float32 [4096], P('tensor'), may hold values from -3 to 3
- down_weight: bfloat16 [4096, 1024], P('tensor'), may hold values from -0.09375 to 0.09375
- down_bias: float32 [1024], replicated, may hold values from -3 to 3
- cotangent: bfloat16 [8192, 1024], P('dp'), may hold values from -6 to 6
Outputs:
- layer_output: bfloat16 [8192, 1024], P('dp')
- grad_tokens: bfloat16 [8192, 1024], P('dp')
- grad_attn_gain: float32 [1024], replicated
- grad_attn_shift: float32 [1024], replicated
- grad_qkv_weight: float32 [3, 1024, 1024], P(None, None, 'tensor')
- grad_qv_bias: float32 [2, 1024], P(None, 'tensor')
- grad_out_weight: float32 [1024, 1024], P('tensor')
- grad_out_bias: float32 [1024], replicated
- grad_mlp_gain: float32 [1024], replicated
- grad_mlp_shift: float32 [1024], replicated
- grad_up_weight: float32 [1024, 4096], P(None, 'tensor')
- grad_up_bias: float32 [4096], P('tensor')
- grad_down_weight: float32 [4096, 1024], P('tensor')
- grad_down_bias: float32 [1024], replicated
Inputs may be any that keep to these rules, and one draw needn't show every extreme that they name: `clip_lengths`: row g lists the clips packed, in order, from the first of data group g's 512 rows; the rows after them are padding. In a quarter of the data groups (at least one), chosen by the seed, one clip fills all 512 rows; every other data group holds one clip of 341 to 426 tokens. Unused entries are 0.
All inputs are finite; a program needn't handle non-finite values.
Results may differ from a plain program's by a relative error of at most 0.012.
Values may be sent and summed in bfloat16 or wider, within the bound.
A program may use at most 192 MiB of HBM per device.

v0:
```python
import jax
import jax.numpy as jnp
from jax import lax
from jax.sharding import PartitionSpec as P

HS = 64


eps_norm = 1e-06
neg_big = -1e30


def matmul(left_side, right_side):
    return jnp.dot(left_side, right_side, preferred_element_type=jnp.float32)


def contract_rows(left_side, right_side):
    return lax.dot_general(
        left_side, right_side, (((0,), (0,)), ((), ())), preferred_element_type=jnp.float32
    )


def contract_cols(left_side, right_side):
    return lax.dot_general(
        left_side, right_side, (((1,), (1,)), ((), ())), preferred_element_type=jnp.float32
    )


def norm_forward(rows_in, gain, shift):
    row_mean = jnp.mean(rows_in, axis=-1, keepdims=True)
    centred = rows_in - row_mean
    variance = jnp.mean(centred * centred, axis=-1, keepdims=True)
    norm_scale = lax.rsqrt(variance + eps_norm)
    normed = centred * norm_scale
    return (normed, norm_scale, normed * gain + shift)


def norm_backward(grad_rows, normed, norm_scale, gain):
    grad_normed = grad_rows * gain
    mean_one = jnp.mean(grad_normed, axis=-1, keepdims=True)
    mean_two = jnp.mean(grad_normed * normed, axis=-1, keepdims=True)
    grad_in = norm_scale * (grad_normed - mean_one - normed * mean_two)
    return (grad_in, jnp.sum(grad_rows * normed, axis=0), jnp.sum(grad_rows, axis=0))


def gelu_parts(pre_act):
    normal_cdf = 0.5 * (1.0 + jax.scipy.special.erf(pre_act * 0.7071067811865476))
    normal_pdf = jnp.exp(-0.5 * pre_act * pre_act) * 0.3989422804014327
    return (pre_act * normal_cdf, normal_cdf + pre_act * normal_pdf)


def segment_rows(clip_lengths, length):
    clip_ends = jnp.cumsum(clip_lengths[0])
    row_index = jnp.arange(length, dtype=jnp.int32)
    return jnp.sum((row_index[:, None] >= clip_ends[None, :]).astype(jnp.int32), axis=1)


def attention_forward(queries, keys_low, values_low, segments, block_rows):
    length, head_count, head_width = queries.shape
    inv_scale = head_width ** (-0.5)
    block_count = length // block_rows

    def one_block(inputs):
        query_block, seg_block = inputs
        products = jnp.einsum(
            "qhd,khd->hqk", query_block, keys_low, preferred_element_type=jnp.float32
        )
        same_clip = seg_block[:, None] == segments[None, :]
        scores = jnp.where(same_clip[None], products * inv_scale, neg_big)
        row_max = jnp.max(scores, axis=2, keepdims=True)
        weights = jnp.exp(scores - row_max)
        row_total = jnp.sum(weights, axis=2, keepdims=True)
        weights_low = (weights / row_total).astype(jnp.bfloat16)
        attended = jnp.einsum(
            "hqk,khd->qhd", weights_low, values_low, preferred_element_type=jnp.float32
        )
        return (attended, (row_max + jnp.log(row_total))[:, :, 0])

    attended, log_totals = lax.map(
        one_block,
        (
            queries.reshape(block_count, block_rows, head_count, head_width),
            segments.reshape(block_count, block_rows),
        ),
    )
    return (attended.reshape(length, head_count * head_width), log_totals)


def attention_backward(
    queries, keys_low, values_low, segments, log_totals, grad_attended, block_rows
):
    length, head_count, head_width = queries.shape
    inv_scale = head_width ** (-0.5)
    block_count = length // block_rows

    def one_block(carried, inputs):
        grad_keys, grad_values = carried
        query_block, seg_block, total_block, grad_block = inputs
        products = jnp.einsum(
            "qhd,khd->hqk", query_block, keys_low, preferred_element_type=jnp.float32
        )
        same_clip = seg_block[:, None] == segments[None, :]
        scores = jnp.where(same_clip[None], products * inv_scale, neg_big)
        probabilities = jnp.exp(scores - total_block[:, :, None])
        grad_probs = jnp.einsum(
            "qhd,khd->hqk", grad_block, values_low, preferred_element_type=jnp.float32
        )
        row_inner = jnp.sum(probabilities * grad_probs, axis=2, keepdims=True)
        grad_scores = (probabilities * (grad_probs - row_inner) * inv_scale).astype(jnp.bfloat16)
        grad_queries = jnp.einsum(
            "hqk,khd->qhd", grad_scores, keys_low, preferred_element_type=jnp.float32
        )
        grad_keys = grad_keys + jnp.einsum(
            "hqk,qhd->khd", grad_scores, query_block, preferred_element_type=jnp.float32
        )
        grad_values = grad_values + jnp.einsum(
            "hqk,qhd->khd",
            probabilities.astype(jnp.bfloat16),
            grad_block,
            preferred_element_type=jnp.float32,
        )
        return ((grad_keys, grad_values), grad_queries)

    zero_grads = jnp.zeros((length, head_count, head_width), jnp.float32)
    shape_four = (block_count, block_rows, head_count, head_width)
    (grad_keys, grad_values), grad_queries = lax.scan(
        one_block,
        (zero_grads, zero_grads),
        (
            queries.reshape(shape_four),
            segments.reshape(block_count, block_rows),
            log_totals,
            grad_attended.reshape(shape_four),
        ),
    )
    flat_shape = (length, head_count * head_width)
    return (
        grad_queries.reshape(flat_shape),
        grad_keys.reshape(flat_shape),
        grad_values.reshape(flat_shape),
    )


def mlp_summed(down_grad, up_grad):
    return (down_grad, up_grad)


def local(
    tokens,
    clip_lengths,
    attn_gain,
    attn_shift,
    qkv_weight,
    qv_bias,
    out_weight,
    out_bias,
    mlp_gain,
    mlp_shift,
    up_weight,
    up_bias,
    down_weight,
    down_bias,
    cotangent,
):
    length = tokens.shape[0]
    local_cols = qkv_weight.shape[2]
    head_count = local_cols // HS
    block_rows = min(512, length)
    segments = segment_rows(clip_lengths, length)
    inputs = tokens.astype(jnp.float32)
    normed_one, scale_one, shifted_one = norm_forward(inputs, attn_gain, attn_shift)
    first_low = shifted_one.astype(jnp.bfloat16)
    head_shape = (length, head_count, HS)
    queries = (
        (matmul(first_low, qkv_weight[0]) + qv_bias[0]).astype(jnp.bfloat16).reshape(head_shape)
    )
    keys_low = matmul(first_low, qkv_weight[1]).astype(jnp.bfloat16).reshape(head_shape)
    values_low = (
        (matmul(first_low, qkv_weight[2]) + qv_bias[1]).astype(jnp.bfloat16).reshape(head_shape)
    )
    attended, log_totals = attention_forward(queries, keys_low, values_low, segments, block_rows)
    attended_low = attended.astype(jnp.bfloat16)
    attn_part = matmul(attended_low, out_weight)
    attn_sum = lax.psum(attn_part, "tensor")
    resid = inputs + attn_sum + out_bias
    normed_two, scale_two, shifted_two = norm_forward(resid, mlp_gain, mlp_shift)
    second_low = shifted_two.astype(jnp.bfloat16)
    pre_act = matmul(second_low, up_weight) + up_bias
    activated, gelu_slope = gelu_parts(pre_act)
    hidden_low = activated.astype(jnp.bfloat16)
    hidden_low, gelu_slope, mlp_part = (hidden_low, gelu_slope, matmul(hidden_low, down_weight))
    mlp_sum = lax.psum(mlp_part.astype(jnp.bfloat16), "tensor").astype(jnp.float32)
    layer_output = (resid + mlp_sum + down_bias).astype(jnp.bfloat16)
    down_grad = contract_rows(hidden_low, cotangent)
    grad_hidden = contract_cols(cotangent, down_weight)
    grad_pre = (grad_hidden * gelu_slope).astype(jnp.bfloat16)
    up_bias_grad = jnp.sum(grad_pre.astype(jnp.float32), axis=0)
    up_grad = contract_rows(second_low, grad_pre)
    back_part = contract_cols(grad_pre, up_weight)
    mlp_pair = mlp_summed(down_grad, up_grad)
    mlp_pair, up_bias_grad, second_part = (mlp_pair, up_bias_grad, back_part)
    second_sum = lax.psum(second_part, "tensor")
    norm_two_grad, mlp_gain_grad, mlp_shift_grad = norm_backward(
        second_sum, normed_two, scale_two, mlp_gain
    )
    cot_full = cotangent.astype(jnp.float32)
    resid_grad = cot_full + norm_two_grad
    out_bias_grad = jnp.sum(resid_grad, axis=0)
    down_bias_grad = jnp.sum(cot_full, axis=0)
    branch_low = resid_grad.astype(jnp.bfloat16)
    out_grad = contract_rows(attended_low, branch_low)
    grad_attended = contract_cols(branch_low, out_weight).astype(jnp.bfloat16).reshape(head_shape)
    grad_queries, grad_keys, grad_values = attention_backward(
        queries, keys_low, values_low, segments, log_totals, grad_attended, block_rows
    )
    query_low = grad_queries.astype(jnp.bfloat16)
    key_low = grad_keys.astype(jnp.bfloat16)
    value_low = grad_values.astype(jnp.bfloat16)
    qv_grad = jnp.stack(
        [
            jnp.sum(query_low.astype(jnp.float32), axis=0),
            jnp.sum(value_low.astype(jnp.float32), axis=0),
        ]
    )
    qkv_grad = jnp.stack(
        [
            contract_rows(first_low, query_low),
            contract_rows(first_low, key_low),
            contract_rows(first_low, value_low),
        ]
    )
    back_part = (
        contract_cols(query_low, qkv_weight[0])
        + contract_cols(key_low, qkv_weight[1])
        + contract_cols(value_low, qkv_weight[2])
    )
    out_grad, qv_grad, qkv_grad, first_part = (out_grad, qv_grad, qkv_grad, back_part)
    first_sum = lax.psum(first_part, "tensor")
    norm_one_grad, attn_gain_grad, attn_shift_grad = norm_backward(
        first_sum, normed_one, scale_one, attn_gain
    )
    grad_tokens = (resid_grad + norm_one_grad).astype(jnp.bfloat16)
    qkv_piece, out_piece, up_piece, down_piece = (
        lax.psum_scatter(qkv_grad.reshape(-1), "dp", scatter_dimension=0, tiled=True),
        lax.psum_scatter(out_grad.reshape(-1), "dp", scatter_dimension=0, tiled=True),
        lax.psum_scatter(mlp_pair[1].reshape(-1), "dp", scatter_dimension=0, tiled=True),
        lax.psum_scatter(mlp_pair[0].reshape(-1), "dp", scatter_dimension=0, tiled=True),
    )
    qkv_flat, out_flat, up_flat, down_flat = (
        lax.all_gather(qkv_piece, "dp", axis=0, tiled=True),
        lax.all_gather(out_piece, "dp", axis=0, tiled=True),
        lax.all_gather(up_piece, "dp", axis=0, tiled=True),
        lax.all_gather(down_piece, "dp", axis=0, tiled=True),
    )
    (
        attn_gain_sum,
        attn_shift_sum,
        qv_sum,
        out_bias_sum,
        mlp_gain_sum,
        mlp_shift_sum,
        up_bias_sum,
        down_bias_sum,
    ) = lax.psum(
        (
            attn_gain_grad,
            attn_shift_grad,
            qv_grad,
            out_bias_grad,
            mlp_gain_grad,
            mlp_shift_grad,
            up_bias_grad,
            down_bias_grad,
        ),
        "dp",
    )
    return (
        layer_output,
        grad_tokens,
        attn_gain_sum,
        attn_shift_sum,
        qkv_flat.reshape(qkv_weight.shape),
        qv_sum,
        out_flat.reshape(out_weight.shape),
        out_bias_sum,
        mlp_gain_sum,
        mlp_shift_sum,
        up_flat.reshape(up_weight.shape),
        up_bias_sum,
        down_flat.reshape(down_weight.shape),
        down_bias_sum,
    )


def solution(mesh):
    placed = (
        P("dp", None),
        P("dp", None),
        P(),
        P(),
        P(None, None, "tensor"),
        P(None, "tensor"),
        P("tensor", None),
        P(),
        P(),
        P(),
        P(None, "tensor"),
        P("tensor"),
        P("tensor", None),
        P(),
        P("dp", None),
    )
    return jax.shard_map(
        local,
        mesh=mesh,
        in_specs=placed,
        out_specs=(
            P("dp", None),
            P("dp", None),
            P(),
            P(),
            P(None, None, "tensor"),
            P(None, "tensor"),
            P("tensor", None),
            P(),
            P(),
            P(),
            P(None, "tensor"),
            P("tensor"),
            P("tensor", None),
            P(),
        ),
        check_vma=False,
    )
```

profile of v0, /device:TPU:0, one launch (start us, length us, event | category | flops | bytes accessed | tf_op | source)
XLA Modules:
  0.0 1057.3 jit_solution(12182547543116176940)
XLA Ops:
  7.3 0.8 fusion.107
  8.1 1.4 convert_reduce_fusion.1
  9.6 1.6 fusion.53
  11.2 2.2 convolution_convert_fusion.2
  13.4 2.4 fusion.55
  16.3 2.2 fusion.56
  18.5 1.5 fusion.3
  20.1 1.7 fusion.2
  21.8 1.6 copy-done.2
  23.5 2.5 fusion.57
  26.0 0.8 copy-done.7
  26.8 2.0 fusion.110
  29.1 65.5 %all-reduce.12.cloned.1.call-done = f32[512,1024]{1,0:T(8,128)} async-done(((f32[512,1024]{1,0:T(8,128)}), f32[512,1024]{1,0:T(8,128)}) %all-reduce.12.cloned.1.call-update) | async-done | bytes 2097168 | tf_op jit(solution)/shard_map/psum | solution.py:184
  94.6 2.4 fusion.105
  97.0 0.3 multiply_reduce_fusion.3
  97.4 0.4 copy-done.27
  98.0 4.2 multiply_convert_fusion.1
  102.2 3.8 convert_reduce_fusion
  106.1 1.3 copy-done.36
  107.4 3.7 fusion.111
  111.4 4.2 convolution_bitcast_fusion.1
  115.6 5.4 copy.47
  121.0 3.3 convolution_convert_fusion
  124.4 4.3 convolution_bitcast_fusion
  128.7 5.3 copy.48
  134.0 40.2 %all-reduce.16.cloned.1.call-done = f32[512,1024]{1,0:T(8,128)} async-done(((f32[512,1024]{1,0:T(8,128)}), f32[512,1024]{1,0:T(8,128)}) %all-reduce.16.cloned.1.call-update) | async-done | bytes 2097168 | tf_op jit(solution)/shard_map/psum | solution.py:202
  174.2 2.4 multiply_reduce_fusion.1
  176.6 40.5 %all-reduce.14.cloned.1.call-done = bf16[512,1024]{1,0:T(8,128)(2,1)} async-done(((bf16[512,1024]{1,0:T(8,128)(2,1)}), bf16[512,1024]{1,0:T(8,128)(2,1)}) %all-reduce.14.cloned.1.call-update) | async-done | bytes 1048592 | tf_op jit(solution)/shard_map/psum | solution.py:192
  217.2 4.6 fusion.104
  221.8 0.7 convolution_convert_fusion.1
  222.5 0.8 copy-done.9
  223.3 4.7 fusion.112
  228.0 14.1 %convert_reduce_fusion.4 = (f32[8,64]{1,0:T(8,128)S(1)}, bf16[8,64,512]{2,1,0:T(8,128)(2,1)}) fusion(bf16[512,8,64]{0,2,1:T(8,128)(2,1)S(1)} %bitcast.93, f32[8,512,512]{1,2,0:T(8,128)} %fusion.112, f32[8,512,512]{1,2,0:T(8,128)} %copy-done.2, f32[8,512]{1,0:T(8,128)S(1)} %log_add_fusion, pred[512,512]{0,1:T(8,128)(4,1)S(1)} %broadcast_compare_fusion), kind=kOutput, calls=%fused_computation.91 | convolution fusion | flops 292294656 | bytes 18106368 | tf_op jit(solution)/shard_map/while/body/eval_jaxpr/hqk,khd->qhd/dot_general | solution.py:110
  242.1 14.4 %fusion.64 = bf16[8,64,512]{2,1,0:T(8,128)(2,1)} fusion(bf16[512,8,64]{0,2,1:T(8,128)(2,1)S(1)} %bitcast.97, f32[8,512,512]{1,2,0:T(8,128)} %fusion.112, f32[8,512,512]{1,2,0:T(8,128)} %copy-done.2, f32[8,512]{1,0:T(8,128)S(1)} %log_add_fusion, pred[512,512]{0,1:T(8,128)(4,1)S(1)} %broadcast_compare_fusion), kind=kOutput, calls=%fused_computation.79 | convolution fusion | flops 291770880 | bytes 18104320 | tf_op jit(solution)/shard_map/while/body/eval_jaxpr/hqk,qhd->khd/dot_general | solution.py:113
  256.5 5.7 convert_reduce_fusion.3
  262.2 0.7 convolution_bitcast_fusion.2
  262.9 0.6 copy-done.5
  263.6 1.0 convolution_bitcast_fusion.3
  264.6 1.0 convolution_bitcast_fusion.4
  265.7 1.0 convolution_bitcast_fusion.5
  266.6 0.7 pad_maximum_fusion
  267.4 4.3 copy.45
  271.7 1.8 copy.46
  273.6 2.3 fusion.70
  276.0 0.8 fusion.67
  277.1 2.1 add_add_fusion
  279.2 0.6 copy-done.34
  279.8 0.6 dynamic-slice.1
  281.0 435.3 %all-reduce.20.cloned.1.call-done = (f32[1572864]{0:T(1024)}, f32[524288]{0:T(1024)}, f32[2097152]{0:T(1024)}, f32[2097152]{0:T(1024)}) async-done(((f32[1572864]{0:T(1024)}, f32[524288]{0:T(1024)}, f32[2097152]{0:T(1024)}, f32[2097152]{0:T(1024)}), (f32[1572864]{0:T(1024)}, f32[524288]{0:T(1024)}, f32[2097152]{0:T(1024)}, f32[2097152]{0:T(1024)})) %all-reduce.20.cloned.1.call-update) | async-done | bytes 25165840
  716.4 1.6 dynamic-slice.4
  718.6 1.8 dynamic-slice.2
  721.1 1.9 dynamic-slice.6
  723.1 1.9 dynamic-slice.8
  725.2 56.7 %all-reduce.18.cloned.1.call-done = f32[512,1024]{1,0:T(8,128)} async-done(((f32[512,1024]{1,0:T(8,128)}), f32[512,1024]{1,0:T(8,128)}) %all-reduce.18.cloned.1.call-update) | async-done | bytes 2097168 | tf_op jit(solution)/shard_map/psum | solution.py:238
  781.9 2.5 fusion.52
  784.4 62.3 %all-reduce.4 = (f32[1024]{0:T(1024)}, f32[1024]{0:T(1024)}, f32[2,512]{1,0:T(2,128)}, f32[1024]{0:T(1024)}, f32[1024]{0:T(1024)}, /*index=5*/f32[1024]{0:T(1024)}, f32[2048]{0:T(1024)}, f32[1024]{0:T(1024)}) all-reduce(f32[1024]{0:T(1024)S(1)} %get-tuple-element.62, ...), channel_id=1, replica_groups=mesh['dp'=16,'tensor'=2] {'dp'}, use_global_device_ids=true, to_apply=%region_18.19 | all-reduce | flops 9216 | bytes 73728 | tf_op jit(solution)/shard_map/psum | solution.py:264
  846.7 3.3 fusion.51
  850.0 2.7 reshape.203
  852.7 36.9 %all-gather.5.cloned.1.call-done = f32[1572864]{0:T(1024)} async-done(((f32[98304]{0:T(1024)}), f32[1572864]{0:T(1024)}) %all-gather.5.cloned.1.call-update) | async-done | bytes 6291472 | tf_op jit(solution)/shard_map/all_gather | solution.py:250
  889.6 7.1 reshape.201
  896.7 69.2 %all-gather.9.cloned.1.call-done = f32[2097152]{0:T(1024)} async-done(((f32[131072]{0:T(1024)}), f32[2097152]{0:T(1024)}) %all-gather.9.cloned.1.call-update) | async-done | bytes 8388624 | tf_op jit(solution)/shard_map/all_gather | solution.py:252
  965.9 9.3 reshape.205
  975.2 66.0 %all-gather.11.cloned.1.call-done = f32[2097152]{0:T(1024)} async-done(((f32[131072]{0:T(1024)}), f32[2097152]{0:T(1024)}) %all-gather.11.cloned.1.call-update) | async-done | bytes 8388624 | tf_op jit(solution)/shard_map/all_gather | solution.py:253
  1041.2 9.3 reshape.207
  (100 shorter events, 2.6 us)
Async XLA Ops:
  7.2 19.6 %copy-start = (bf16[512,1024]{1,0:T(8,128)(2,1)S(1)}, bf16[512,1024]{1,0:T(8,128)(2,1)}, u32[]{:S(2)}) copy-start(bf16[512,1024]{1,0:T(8,128)(2,1)} %param.21) | copy-start | bytes 3145732
  7.2 4.0 copy-start.4
  7.2 4.0 copy-start.32
  7.2 4.0 copy-start.24
  7.2 87.4 %all-reduce.12.cloned.1.call-start = ((), (), s32[]{:S(2)}) async-start(), calls=%async_computation | async-start | bytes 4194304 | tf_op jit(solution)/shard_map/psum | solution.py:184
  13.4 5.1 copy-start.12
  13.4 2.4 copy-start.33
  15.8 6.0 copy-start.14
  18.5 1.5 copy-start.16
  20.1 3.4 copy-start.2
  26.0 0.8 copy-start.7
  26.8 67.9 %copy-start.26 = (f32[1024]{0:T(1024)S(1)}, f32[1024]{0:T(1024)}, u32[]{:S(2)}) copy-start(f32[1024]{0:T(1024)} %param.22) | copy-start | bytes 12292
  28.8 145.3 %all-reduce.16.cloned.1.call-start = ((), (), s32[]{:S(2)}) async-start(), calls=%async_computation.2 | async-start | bytes 4194304 | tf_op jit(solution)/shard_map/psum | solution.py:202
  94.6 3.1 copy-start.27
  97.0 77.2 %copy-start.3 = (f32[512,1024]{1,0:T(8,128)}, f32[512,1024]{1,0:T(8,128)S(1)}, u32[]{:S(2)}) copy-start(f32[512,1024]{1,0:T(8,128)S(1)} %get-tuple-element.94) | copy-start | bytes 6291460
  97.0 0.9 copy-start.23
  97.0 0.9 copy-start.30
  97.0 1.0 copy-start.31
  98.0 4.2 copy-start.11
  98.0 4.2 copy-start.28
  106.0 1.4 copy-start.36
  111.1 106.0 %all-reduce.14.cloned.1.call-start = ((), (), s32[]{:S(2)}) async-start(), calls=%async_computation.1 | async-start | bytes 2097152 | tf_op jit(solution)/shard_map/psum | solution.py:192
  115.6 5.4 copy-start.29
  115.6 5.4 copy-start.35
  124.4 592.0 %all-reduce.20.cloned.1.call-start = ((), (), s32[]{:S(2)}) async-start(), calls=%async_computation.8 | async-start | bytes 50331648
  134.0 83.1 %copy-start.25 = (f32[1024]{0:T(1024)S(1)}, f32[1024]{0:T(1024)}, u32[]{:S(2)}) copy-start(f32[1024]{0:T(1024)} %param.28) | copy-start | bytes 12292
  221.7 1.5 copy-start.15
  222.5 0.8 copy-start.9
  223.3 4.7 copy-start.13
  228.0 14.1 %copy-start.17 = (bf16[512,512]{0,1:T(8,128)(2,1)S(1)}, bf16[512,512]{0,1:T(8,128)(2,1)}, u32[]{:S(2)}) copy-start(bf16[512,512]{0,1:T(8,128)(2,1)} %copy-done.16) | copy-start | bytes 1572868
  242.1 14.4 %copy-start.10 = (bf16[512,512]{0,1:T(8,128)(2,1)S(1)}, bf16[512,512]{0,1:T(8,128)(2,1)}, u32[]{:S(2)}) copy-start(bf16[512,512]{0,1:T(8,128)(2,1)} %copy-done.9) | copy-start | bytes 1572868
  256.4 5.7 copy-start.8
  262.1 0.8 copy-start.21
  262.2 1.4 copy-start.5
  263.6 1.0 copy-start.19
  264.6 1.0 copy-start.18
  273.5 508.4 %all-reduce.18.cloned.1.call-start = ((), (), s32[]{:S(2)}) async-start(), calls=%async_computation.3 | async-start | bytes 4194304 | tf_op jit(solution)/shard_map/psum | solution.py:238
  273.5 2.4 copy-start.6
  273.6 2.5 copy-start.20
  276.0 1.0 copy-start.22
  279.1 0.7 copy-start.34
  279.2 570.9 %all-gather.7.cloned.1.call-start = ((), (), s32[]{:S(2)}) async-start(), calls=%async_computation.5 | async-start | bytes 2228224 | tf_op jit(solution)/shard_map/all_gather | solution.py:251
  717.9 171.6 %all-gather.5.cloned.1.call-start = ((), (), s32[]{:S(2)}) async-start(), calls=%async_computation.4 | async-start | bytes 6684672 | tf_op jit(solution)/shard_map/all_gather | solution.py:250
  720.4 245.4 %all-gather.9.cloned.1.call-start = ((), (), s32[]{:S(2)}) async-start(), calls=%async_computation.6 | async-start | bytes 8912896 | tf_op jit(solution)/shard_map/all_gather | solution.py:252
  723.0 318.2 %all-gather.11.cloned.1.call-start = ((), (), s32[]{:S(2)}) async-start(), calls=%async_computation.7 | async-start | bytes 8912896 | tf_op jit(solution)/shard_map/all_gather | solution.py:253
  1041.2 9.3 copy-start.1
Sparse Core Ops, SparseCore 0:
  29.0 65.6 all-reduce.11
  111.2 62.9 all-reduce.15
  177.1 40.0 all-reduce.13
  273.6 442.6 all-reduce.19
  719.2 62.6 all-reduce.17
  784.5 41.4 all-gather.6
  828.8 60.6 all-gather.4
  892.3 73.4 all-gather.8
  968.0 73.1 all-gather.10
where the time goes:
time: 1070 us; the launch traced here: 1060 us
  waiting for transfers between devices  810 us (76%)
  matrix products  84.7 us (8%)
  blocking collectives  62.3 us (6%)
  local copies, waits for them, and re-layouts  61 us (6%)
  other arithmetic  21.6 us (2%)
  between operations  16.4 us (2%)
    unnamed x10, waiting for transfers between devices  435 us
    all_gather x1, waiting for transfers between devices, local(): lax.all_gather(up_piece, 'dp', axis=0, tiled=True)  69.2 us
    all_gather x1, waiting for transfers between devices, local(): lax.all_gather(down_piece, 'dp', axis=0, tiled=True)  66 us
    psum x1, waiting for transfers between devices, local(): attn_sum = lax.psum(attn_part, 'tensor')  65.5 us
    psum x1, blocking collectives, local(): lax.psum((attn_gain_grad, attn_shift_grad, qv_grad, out_bias_grad, mlp_ga...  62.3 us
    psum x1, waiting for transfers between devices, local(): first_sum = lax.psum(first_part, 'tensor')  56.7 us
    psum x1, waiting for transfers between devices, local(): lax.psum(mlp_part.astype(jnp.bfloat16), 'tensor').astype(jnp.float32)  40.5 us
    psum x1, waiting for transfers between devices, local(): second_sum = lax.psum(second_part, 'tensor')  40.2 us
  transfers between devices with their start and end apart: 9, of which 8 were waited for; matrix products, arithmetic and copies ran while one was open for 6% of the time, Pallas kernels for 0%

commit v1 on v0

--- a/solution.py
+++ b/solution.py
@@ -1,6 +1,328 @@
 import jax
 import jax.numpy as jnp
 from jax import lax
+from jax.experimental import pallas as pl
+from jax.experimental.pallas import tpu as pltpu
+
+MESH = pl.DeviceIdType.MESH
+bf16, f32 = jnp.bfloat16, jnp.float32
+CELL = 16
+NSA = 6
+STAGES = 6
+
+
+def place():
+    at = lax.axis_index("dp")
+    base = (at // CELL) * CELL
+    inner = at - base
+    z = inner // 4
+    y = (inner // 2) % 2
+    core = inner % 2
+    return base, z, y, core
+
+
+class Summer:
+    def __init__(self, loc_a, loc_b, bufs, out_a, out_b, sems):
+        self.loc_a, self.loc_b = loc_a, loc_b
+        (self.a1, self.a2, self.a3, self.b1, self.b2, self.b3) = bufs
+        self.out_a, self.out_b = out_a, out_b
+        self.as_, self.ar_, self.bs_, self.br_, self.ls_ = sems
+        self.na = loc_a.shape[0]
+        self.nb = loc_b.shape[0]
+        self.ha = loc_a.shape[1] // 2
+        self.hb = loc_b.shape[1] // 2
+        base, z, y, core = place()
+        self.y, self.core = y, core
+        self.outer = jnp.logical_or(z == 0, z == 3)
+        self.mid = jnp.logical_not(self.outer)
+        self.mine = jnp.where(z >= 2, 1, 0)
+        across = 3 - z
+        toward = jnp.where(z < 2, 1 - z, 5 - z)
+        tensor = lax.axis_index("tensor")
+
+        def dev(zz, yy, cc):
+            return (base + zz * 4 + yy * 2 + cc, tensor)
+
+        self.to_sib = dev(z, y, 1 - core)
+        self.to_y = dev(z, 1 - y, core)
+        self.to_x = None
+        self.to_mid = dev(across, y, core)
+        self.to_z = dev(toward, y, core)
+
+    def la(self, i, h):
+        return self.loc_a.at[i, pl.ds(pl.multiple_of(h * self.ha, self.ha), self.ha), :]
+
+    def lb(self, i, h):
+        return self.loc_b.at[i, pl.ds(pl.multiple_of(h * self.hb, self.hb), self.hb), :]
+
+    def oa(self, i, h, core):
+        return self.out_a.at[i, core, pl.ds(pl.multiple_of(h * self.ha, self.ha), self.ha), :]
+
+    def ob(self, i, h, core):
+        w = self.loc_b.shape[2]
+        return self.out_b.at[
+            i,
+            pl.ds(pl.multiple_of(h * self.hb, self.hb), self.hb),
+            pl.ds(pl.multiple_of(core * w, w), w),
+        ]
+
+    def ca(self, i, kind, recv, src, dst, to):
+        return pltpu.make_async_remote_copy(
+            src, dst, self.as_.at[i, kind], self.ar_.at[i, recv], device_id=to, device_id_type=MESH
+        )
+
+    def cb(self, i, kind, recv, src, dst, to):
+        return pltpu.make_async_remote_copy(
+            src, dst, self.bs_.at[i, kind], self.br_.at[i, recv], device_id=to, device_id_type=MESH
+        )
+
+    def a_y(self, i):
+        return self.ca(i, 0, 0, self.la(i, 1 - self.y), self.a1.at[i], self.to_y)
+
+    def a_in(self, i):
+        return self.ca(i, 1, 1, self.la(i, self.y), self.a2.at[i], self.to_z)
+
+    def a_mid(self, i):
+        return self.ca(i, 1, 2, self.la(i, self.y), self.a3.at[i], self.to_mid)
+
+    def a_out(self, i):
+        return self.ca(i, 2, 3, self.a2.at[i], self.oa(i, self.y, self.core), self.to_z)
+
+    def a_done(self, i, kind, recv, src, to):
+        return self.ca(i, kind, recv, src, self.oa(i, self.y, self.core), to)
+
+    def a_keep(self, i):
+        return pltpu.make_async_copy(self.a2.at[i], self.oa(i, self.y, self.core), self.ls_.at[0, i])
+
+    def a_fwd(self, i):
+        o = self.oa(i, 1 - self.y, self.core)
+        return self.ca(i, 5, 6, o, o, self.to_sib)
+
+    def step_a(self, i, stage):
+        y = self.y
+        if stage == 0:
+            self.a_y(i).start()
+        elif stage == 1:
+            self.a_y(i).wait_recv()
+            v = self.la(i, y)
+            v[...] = (v[...].astype(f32) + self.a1[i].astype(f32)).astype(bf16)
+
+            @pl.when(self.outer)
+            def _():
+                self.a_in(i).start()
+        elif stage == 2:
+            @pl.when(self.mid)
+            def _():
+                self.a_in(i).wait_recv()
+                v = self.la(i, y)
+                v[...] = (v[...].astype(f32) + self.a2[i].astype(f32)).astype(bf16)
+                self.a_mid(i).start()
+        elif stage == 3:
+            @pl.when(self.mid)
+            def _():
+                self.a_mid(i).wait_recv()
+                self.a2[i] = (self.la(i, y)[...].astype(f32) + self.a3[i].astype(f32)).astype(bf16)
+                self.a_out(i).start()
+                src = self.a2.at[i]
+                self.a_done(i, 3, 4, src, self.to_y).start()
+                self.a_done(i, 4, 5, src, self.to_sib).start()
+                self.a_keep(i).start()
+        elif stage == 4:
+            @pl.when(self.outer)
+            def _():
+                self.a_out(i).wait_recv()
+                src = self.oa(i, y, self.core)
+                self.a_done(i, 3, 4, src, self.to_y).start()
+                self.a_done(i, 4, 5, src, self.to_sib).start()
+        elif stage == 5:
+            self.a_done(i, 3, 4, self.oa(i, y, self.core), self.to_y).wait_recv()
+            self.a_fwd(i).start()
+
+    def end_a(self, i):
+        src = self.a2.at[i]
+        self.a_y(i).wait_send()
+        self.a_in(i).wait_send()
+
+        @pl.when(self.mid)
+        def _():
+            self.a_out(i).wait_send()
+            self.a_keep(i).wait()
+
+        self.a_done(i, 3, 4, src, self.to_y).wait_send()
+        self.a_done(i, 4, 5, src, self.to_sib).wait_send()
+        self.a_fwd(i).wait_send()
+        self.a_done(i, 4, 5, src, self.to_sib).wait_recv()
+        self.a_fwd(i).wait_recv()
+
+    def b_in(self, i):
+        return self.cb(i, 0, 0, self.loc_b.at[i], self.b1.at[i], self.to_z)
+
+    def b_mid(self, i):
+        return self.cb(i, 0, 1, self.lb(i, 1 - self.mine), self.b2.at[i], self.to_mid)
+
+    def b_y(self, i):
+        return self.cb(i, 1, 2, self.lb(i, self.mine), self.b3.at[i], self.to_y)
+
+    def fin_b(self, i):
+        return self.b1.at[i, pl.ds(0, self.hb), :]
+
+    def b_done(self, i, kind, recv, src, h, to):
+        return self.cb(i, kind, recv, src, self.ob(i, h, self.core), to)
+
+    def b_keep(self, i):
+        return pltpu.make_async_copy(
+            self.fin_b(i), self.ob(i, self.mine, self.core), self.ls_.at[1, i]
+        )
+
+    def step_b(self, i, stage):
+        mine, core = self.mine, self.core
+        if stage == 0:
+            @pl.when(self.outer)
+            def _():
+                self.b_in(i).start()
+        elif stage == 1:
+            @pl.when(self.mid)
+            def _():
+                self.b_in(i).wait_recv()
+                self.loc_b[i] = (self.loc_b[i].astype(f32) + self.b1[i].astype(f32)).astype(bf16)
+                self.b_mid(i).start()
+        elif stage == 2:
+            @pl.when(self.mid)
+            def _():
+                self.b_mid(i).wait_recv()
+                v = self.lb(i, mine)
+                v[...] = (v[...].astype(f32) + self.b2[i].astype(f32)).astype(bf16)
+                self.b_y(i).start()
+        elif stage == 3:
+            @pl.when(self.mid)
+            def _():
+                self.b_y(i).wait_recv()
+                fin = self.fin_b(i)
+                fin[...] = (self.lb(i, mine)[...].astype(f32) + self.b3[i].astype(f32)).astype(bf16)
+                self.b_done(i, 2, 4, fin, mine, self.to_mid).start()
+                self.b_done(i, 3, 3, fin, mine, self.to_z).start()
+                self.b_done(i, 4, 5, fin, mine, self.to_sib).start()
+                self.b_keep(i).start()
+        elif stage == 4:
+            @pl.when(self.mid)
+            def _():
+                o = self.ob(i, 1 - mine, core)
+                self.b_done(i, 2, 4, o, 1 - mine, self.to_mid).wait_recv()
+                self.b_done(i, 5, 4, o, 1 - mine, self.to_z).start()
+                self.b_done(i, 6, 6, o, 1 - mine, self.to_sib).start()
+
+            @pl.when(self.outer)
+            def _():
+                o = self.ob(i, mine, core)
+                self.b_done(i, 3, 3, o, mine, self.to_z).wait_recv()
+                self.b_done(i, 4, 5, o, mine, self.to_sib).start()
+        elif stage == 5:
+            @pl.when(self.outer)
+            def _():
+                o = self.ob(i, 1 - mine, core)
+                self.b_done(i, 5, 4, o, 1 - mine, self.to_z).wait_recv()
+                self.b_done(i, 6, 6, o, 1 - mine, self.to_sib).start()
+
+    def end_b(self, i):
+        fin = self.fin_b(i)
+        mine = self.mine
+
+        @pl.when(self.outer)
+        def _():
+            self.b_in(i).wait_send()
+
+        @pl.when(self.mid)
+        def _():
+            self.b_mid(i).wait_send()
+            self.b_y(i).wait_send()
+            self.b_done(i, 2, 4, fin, mine, self.to_mid).wait_send()
+            self.b_done(i, 3, 3, fin, mine, self.to_z).wait_send()
+            self.b_done(i, 5, 4, fin, mine, self.to_z).wait_send()
+            self.b_keep(i).wait()
+
+        self.b_done(i, 4, 5, fin, mine, self.to_sib).wait_send()
+        self.b_done(i, 6, 6, fin, mine, self.to_sib).wait_send()
+        self.b_done(i, 4, 5, fin, mine, self.to_sib).wait_recv()
+        self.b_done(i, 6, 6, fin, mine, self.to_sib).wait_recv()
+
+    def step(self, t):
+        for stage in range(STAGES):
+            i = t - stage
+
+            @pl.when(jnp.logical_and(i >= 0, i < self.na))
+            def _():
+                self.step_a(i, stage)
+
+            @pl.when(jnp.logical_and(i >= 0, i < self.nb))
+            def _():
+                self.step_b(i, stage)
+
+    def steps(self, lo, hi):
+        def body(t, _):
+            self.step(t)
+            return 0
+
+        lax.fori_loop(lo, hi, body, 0)
+
+    def end(self):
+        def body_a(i, _):
+            self.end_a(i)
+            return 0
+
+        def body_b(i, _):
+            self.end_b(i)
+            return 0
+
+        lax.fori_loop(0, self.na, body_a, 0)
+        lax.fori_loop(0, self.nb, body_b, 0)
+
+
+def scratch_of(na, ra, wa, nb, rb, wb):
+    return [
+        pltpu.VMEM((na, ra // 2, wa), bf16),
+        pltpu.VMEM((na, ra // 2, wa), bf16),
+        pltpu.VMEM((na, ra // 2, wa), bf16),
+        pltpu.VMEM((nb, rb, wb), bf16),
+        pltpu.VMEM((nb, rb // 2, wb), bf16),
+        pltpu.VMEM((nb, rb // 2, wb), bf16),
+        pltpu.SemaphoreType.DMA((na, 6)),
+        pltpu.SemaphoreType.DMA((na, 7)),
+        pltpu.SemaphoreType.DMA((nb, 7)),
+        pltpu.SemaphoreType.DMA((nb, 7)),
+        pltpu.SemaphoreType.DMA((2, max(na, nb))),
+    ]
+
+
+def sum_kernel(in_a, in_b, out_a, out_b, loc_a, loc_b, a1, a2, a3, b1, b2, b3, as_, ar_, bs_, br_, ls_, lsem):
+    ca = pltpu.make_async_copy(in_a, loc_a, lsem.at[0])
+    cb = pltpu.make_async_copy(in_b, loc_b, lsem.at[1])
+    ca.start()
+    cb.start()
+    s = Summer(loc_a, loc_b, (a1, a2, a3, b1, b2, b3), out_a, out_b, (as_, ar_, bs_, br_, ls_))
+    ca.wait()
+    cb.wait()
+    s.steps(0, max(s.na, s.nb) + STAGES - 1)
+    s.end()
+
+
+def group_sum(in_a, in_b):
+    na, ra, wa = in_a.shape
+    nb, rb, wb = in_b.shape
+    return pl.pallas_call(
+        sum_kernel,
+        out_shape=(
+            jax.ShapeDtypeStruct((na, 2, ra, wa), bf16),
+            jax.ShapeDtypeStruct((nb, rb, 2 * wb), bf16),
+        ),
+        in_specs=[pl.BlockSpec(memory_space=pl.ANY)] * 2,
+        out_specs=[pl.BlockSpec(memory_space=pl.ANY)] * 2,
+        scratch_shapes=[pltpu.VMEM(in_a.shape, bf16), pltpu.VMEM(in_b.shape, bf16)]
+        + scratch_of(na, ra, wa, nb, rb, wb)
+        + [pltpu.SemaphoreType.DMA((2,))],
+        compiler_params=pltpu.CompilerParams(has_side_effects=True, vmem_limit_bytes=56 << 20),
+        name="group_sum",
+    )(in_a, in_b)
+
 from jax.sharding import PartitionSpec as P
 
 HS = 64
@@ -50,7 +372,9 @@
 
 
 def segment_rows(clip_lengths, length):
-    clip_ends = jnp.cumsum(clip_lengths[0])
+    first = clip_lengths[0, 0]
+    second = first + clip_lengths[0, 1]
+    clip_ends = jnp.stack([first, second, second + clip_lengths[0, 2]])
     row_index = jnp.arange(length, dtype=jnp.int32)
     return jnp.sum((row_index[:, None] >= clip_ends[None, :]).astype(jnp.int32), axis=1)
 
@@ -141,8 +465,32 @@
     )
 
 
-def mlp_summed(down_grad, up_grad):
-    return (down_grad, up_grad)
+def over_tensor(part):
+    low = part.astype(jnp.bfloat16)
+    other = lax.ppermute(low, "tensor", [(0, 1), (1, 0)])
+    return low.astype(jnp.float32) + other.astype(jnp.float32)
+
+
+def from_sibling(value):
+    count = lax.axis_size("dp")
+    return lax.ppermute(value, "dp", [(i, i ^ 1) for i in range(count)])
+
+
+def pair_rows(value):
+    core = lax.axis_index("dp") % 2
+    other = from_sibling(value)
+    first = jnp.where(core == 0, value, other)
+    return jnp.concatenate([first, jnp.where(core == 0, other, value)], axis=0)
+
+
+def pair_cols(value, pieces):
+    core = lax.axis_index("dp") % 2
+    rows, cols = value.shape
+    halves = value.reshape(rows, pieces, 2, cols // pieces // 2)
+    mine = jnp.where(core == 0, halves[:, :, 0], halves[:, :, 1])
+    other = from_sibling(jnp.where(core == 0, halves[:, :, 1], halves[:, :, 0]))
+    first = jnp.where(core == 0, mine, other)
+    return jnp.concatenate([first, jnp.where(core == 0, other, mine)], axis=0)
 
 
 def local(
@@ -181,25 +529,29 @@
     attended, log_totals = attention_forward(queries, keys_low, values_low, segments, block_rows)
     attended_low = attended.astype(jnp.bfloat16)
     attn_part = matmul(attended_low, out_weight)
-    attn_sum = lax.psum(attn_part, "tensor")
+    attn_sum = over_tensor(attn_part)
     resid = inputs + attn_sum + out_bias
     normed_two, scale_two, shifted_two = norm_forward(resid, mlp_gain, mlp_shift)
     second_low = shifted_two.astype(jnp.bfloat16)
     pre_act = matmul(second_low, up_weight) + up_bias
     activated, gelu_slope = gelu_parts(pre_act)
     hidden_low = activated.astype(jnp.bfloat16)
-    hidden_low, gelu_slope, mlp_part = (hidden_low, gelu_slope, matmul(hidden_low, down_weight))
-    mlp_sum = lax.psum(mlp_part.astype(jnp.bfloat16), "tensor").astype(jnp.float32)
+    mlp_part = matmul(hidden_low, down_weight)
+    mlp_sum = over_tensor(mlp_part)
     layer_output = (resid + mlp_sum + down_bias).astype(jnp.bfloat16)
-    down_grad = contract_rows(hidden_low, cotangent)
     grad_hidden = contract_cols(cotangent, down_weight)
     grad_pre = (grad_hidden * gelu_slope).astype(jnp.bfloat16)
     up_bias_grad = jnp.sum(grad_pre.astype(jnp.float32), axis=0)
-    up_grad = contract_rows(second_low, grad_pre)
     back_part = contract_cols(grad_pre, up_weight)
-    mlp_pair = mlp_summed(down_grad, up_grad)
-    mlp_pair, up_bias_grad, second_part = (mlp_pair, up_bias_grad, back_part)
-    second_sum = lax.psum(second_part, "tensor")
+    second_part = back_part
+    pieces = hidden_low.shape[1] // 512
+    pair_hidden = pair_cols(hidden_low, pieces)
+    pair_pre = pair_cols(grad_pre, pieces)
+    pair_cot = pair_rows(cotangent)
+    pair_second = pair_rows(second_low)
+    down_grad = jnp.einsum("rph,rd->phd", pair_hidden, pair_cot, preferred_element_type=jnp.float32)
+    up_grad = jnp.einsum("rd,rph->pdh", pair_second, pair_pre, preferred_element_type=jnp.float32)
+    second_sum = over_tensor(second_part)
     norm_two_grad, mlp_gain_grad, mlp_shift_grad = norm_backward(
         second_sum, normed_two, scale_two, mlp_gain
     )
@@ -208,7 +560,9 @@
     out_bias_grad = jnp.sum(resid_grad, axis=0)
     down_bias_grad = jnp.sum(cot_full, axis=0)
     branch_low = resid_grad.astype(jnp.bfloat16)
-    out_grad = contract_rows(attended_low, branch_low)
+    out_grad = jnp.einsum(
+        "rph,rd->phd", pair_cols(attended_low, 1), pair_rows(branch_low), preferred_element_type=jnp.float32
+    )
     grad_attended = contract_cols(branch_low, out_weight).astype(jnp.bfloat16).reshape(head_shape)
     grad_queries, grad_keys, grad_values = attention_backward(
         queries, keys_low, values_low, segments, log_totals, grad_attended, block_rows
@@ -222,11 +576,11 @@
             jnp.sum(value_low.astype(jnp.float32), axis=0),
         ]
     )
-    qkv_grad = jnp.stack(
+    pair_first = pair_rows(first_low)
+    qkv_grad = jnp.concatenate(
         [
-            contract_rows(first_low, query_low),
-            contract_rows(first_low, key_low),
-            contract_rows(first_low, value_low),
+            jnp.einsum("rd,rph->pdh", pair_first, pair_cols(v, 1), preferred_element_type=jnp.float32)
+            for v in (query_low, key_low, value_low)
         ]
     )
     back_part = (
@@ -234,24 +588,29 @@
         + contract_cols(key_low, qkv_weight[1])
         + contract_cols(value_low, qkv_weight[2])
     )
-    out_grad, qv_grad, qkv_grad, first_part = (out_grad, qv_grad, qkv_grad, back_part)
-    first_sum = lax.psum(first_part, "tensor")
+    first_part = back_part
+    first_sum = over_tensor(first_part)
     norm_one_grad, attn_gain_grad, attn_shift_grad = norm_backward(
         first_sum, normed_one, scale_one, attn_gain
     )
     grad_tokens = (resid_grad + norm_one_grad).astype(jnp.bfloat16)
-    qkv_piece, out_piece, up_piece, down_piece = (
-        lax.psum_scatter(qkv_grad.reshape(-1), "dp", scatter_dimension=0, tiled=True),
-        lax.psum_scatter(out_grad.reshape(-1), "dp", scatter_dimension=0, tiled=True),
-        lax.psum_scatter(mlp_pair[1].reshape(-1), "dp", scatter_dimension=0, tiled=True),
-        lax.psum_scatter(mlp_pair[0].reshape(-1), "dp", scatter_dimension=0, tiled=True),
-    )
-    qkv_flat, out_flat, up_flat, down_flat = (
-        lax.all_gather(qkv_piece, "dp", axis=0, tiled=True),
-        lax.all_gather(out_piece, "dp", axis=0, tiled=True),
-        lax.all_gather(up_piece, "dp", axis=0, tiled=True),
-        lax.all_gather(down_piece, "dp", axis=0, tiled=True),
-    )
+    in_a = jnp.concatenate([down_grad, out_grad]).astype(jnp.bfloat16)
+    in_b = jnp.concatenate([up_grad, qkv_grad]).astype(jnp.bfloat16)
+    na, ra, wa = in_a.shape
+    nb, rb, wb = in_b.shape
+    sum_a, sum_b = group_sum(in_a.reshape(na * 2, ra // 2, wa), in_b.reshape(nb * 2, rb // 2, wb))
+    groups = lax.axis_size("dp")
+    if groups > CELL:
+        cells = [[k * CELL + i for k in range(groups // CELL)] for i in range(CELL)]
+        sum_a, sum_b = lax.psum(
+            (sum_a.astype(f32), sum_b.astype(f32)), "dp", axis_index_groups=cells
+        )
+    sum_a = sum_a.reshape(na, 2, 2, ra // 2, wa).transpose(0, 2, 1, 3, 4).reshape(na, 2 * ra, wa)
+    sum_b = sum_b.reshape(nb, rb, 2 * wb)
+    down_flat = sum_a[: na - 1].reshape(-1, wa).astype(jnp.float32)
+    out_flat = sum_a[na - 1].astype(jnp.float32)
+    up_flat = sum_b[: nb - 3].transpose(1, 0, 2).reshape(rb, -1).astype(jnp.float32)
+    qkv_flat = sum_b[nb - 3 :].astype(jnp.float32)
     (
         attn_gain_sum,
         attn_shift_sum,

time: 1070 us -> 469 us (0.44)
  waiting for transfers between devices: 810 us -> 22.1 us
  Pallas kernels: 0 us -> 148 us
  other arithmetic: 21.6 us -> 59 us
  between operations: 16.4 us -> 3.85 us
  local copies, waits for them, and re-layouts: 61 us -> 73.1 us
    unnamed x10 -> x0, waiting for transfers between devices: 435 us -> none
    psum x4 -> x0, waiting for transfers between devices: 203 us -> none  [the longest x1 65.5 us: local(): attn_sum = lax.psum(attn_part, 'tensor')]
    all_gather x4 -> x0, waiting for transfers between devices: 172 us -> none  [the longest x1 69.2 us: local(): lax.all_gather(up_piece, 'dp', axis=0, tiled=True)]
    pallas_call x0 -> x1, Pallas kernels: none -> 148 us  [group_sum(): pl.pallas_call(sum_kernel, out_shape=(jax.ShapeDtypeStruct((na, 2, ra, wa...]
    select_n x0 -> x16, other arithmetic: none -> 22.5 us  [the longest x4 9.81 us: pair_rows(): first = jnp.where(core == 0, value, other)]
    ppermute x0 -> x14, waiting for transfers between devices: none -> 22.1 us  [the longest x4 21.2 us: over_tensor(): other = lax.ppermute(low, 'tensor', [(0, 1), (1, 0)])]
    reshape x4 -> x2, local copies, waits for them, and re-layouts: 28.4 us -> 8.98 us  [pair_cols(): halves = value.reshape(rows, pieces, 2, cols // pieces // 2)]
    slice x0 -> x5, local copies, waits for them, and re-layouts: none -> 17.3 us  [the longest x2 11.1 us: pair_cols(): mine = jnp.where(core == 0, halves[:, :, 0], halves[:, :, 1])]
  transfers between devices with their start and end apart: 9 -> 14, of which waited for: 8 -> 3; matrix products, arithmetic and copies ran while one was open for 6% -> 36% of each run, Pallas kernels for 0% -> 32%
where the time goes in v1:
time: 469 us; the launch traced here: 463 us
  Pallas kernels  148 us (32%)
  matrix products  85.1 us (18%)
  local copies, waits for them, and re-layouts  73.1 us (16%)
  blocking collectives  62.5 us (13%)
  other arithmetic  59 us (13%)
  waiting for transfers between devices  22.1 us (5%)
  starting transfers between devices  8.89 us (2%)
    pallas_call x1, Pallas kernels, group_sum(): pl.pallas_call(sum_kernel, out_shape=(jax.ShapeDtypeStruct((na, 2, ra, wa...  148 us
    psum x1, blocking collectives, local(): lax.psum((attn_gain_grad, attn_shift_grad, qv_grad, out_bias_grad, mlp_ga...  62.5 us
    unnamed x110, local copies, waits for them, and re-layouts  29.2 us
    ppermute x4, waiting for transfers between devices, over_tensor(): other = lax.ppermute(low, 'tensor', [(0, 1), (1, 0)])  21.2 us
    dot_general x6, matrix products, matmul(): return jnp.dot(left_side, right_side, preferred_element_type=jnp.float32)  18.6 us
    dot_general x6, matrix products, contract_cols(): lax.dot_general(left_side, right_side, (((1,), (1,)), ((), ())), preferre...  16.8 us
    dot_general x1, matrix products, one_block(): jnp.einsum('hqk,khd->qhd', grad_scores, keys_low, preferred_element_type=...  14.2 us
    dot_general x1, matrix products, one_block(): jnp.einsum('hqk,qhd->khd', grad_scores, query_block, preferred_element_ty...  13.5 us
  transfers between devices with their start and end apart: 14, of which 3 were waited for; matrix products, arithmetic and copies ran while one was open for 36% of the time, Pallas kernels for 32%

profile of v1, /device:TPU:0, one launch (start us, length us, event | category | flops | bytes accessed | tf_op | source)
XLA Modules:
  0.0 462.9 jit_solution(11725397821747995524)
XLA Ops:
  0.7 1.4 fusion.151
  4.9 1.4 convert_reduce_fusion.1
  6.3 1.6 fusion.53
  8.9 2.7 fusion.46
  11.6 2.0 convolution_convert_fusion.7
  13.6 2.2 fusion.83
  15.8 2.2 fusion.82
  18.0 1.5 fusion.3
  19.6 1.7 fusion.2
  21.3 1.6 copy-done.4
  23.0 3.0 fusion.84
  26.7 3.0 collective-permute-start
  32.2 20.8 %collective-permute-done = bf16[512,1024]{1,0:T(8,128)(2,1)} collective-permute-done((bf16[512,1024]{1,0:T(8,128)(2,1)S(1)}, bf16[512,1024]{1,0:T(8,128)(2,1)}, u32[]{:S(2)}, u32[]{:S(2)}) %collective-permute-start) | collective-permute-done | bytes 1048608 | tf_op jit(solution)/shard_map/ppermute | solution.py:470
  53.0 2.4 fusion.146
  55.8 1.4 add_convert_fusion.2
  57.9 5.4 %multiply_convert_fusion.1 = (bf16[512,2048]{1,0:T(8,128)(2,1)}, f32[512,2048]{1,0:T(8,128)S(1)}) fusion(f32[2048]{0:T(1024)S(1)} %copy-done.48, bf16[512,1024]{1,0:T(8,128)(2,1)} %add_convert_fusion.2, bf16[1024,2048]{1,0:T(8,128)(2,1)S(1)} %copy-done.46), kind=kOutput, calls=%fused_computation.25 | convolution fusion | flops 2153775104 | bytes 11542528 | tf_op jit(solution)/shard_map/dot_general | solution.py:336
  63.4 5.4 %convert_reduce_fusion = (f32[2048]{0:T(1024)S(1)}, bf16[512,2048]{1,0:T(8,128)(2,1)S(1)}) fusion(f32[512,2048]{1,0:T(8,128)S(1)} %get-tuple-element.129, f32[2048]{0:T(1024)S(1)} %copy-done.48, bf16[512,1024]{1,0:T(8,128)(2,1)} %param.29, bf16[2048,1024]{1,0:T(8,128)(2,1)S(1)} %copy-done.47), kind=kOutput, calls=%fused_computation.22 | convolution fusion | flops 2161113088 | bytes 11550720 | tf_op jit(solution)/shard_map/dot_general | solution.py:346
  68.8 1.3 copy-done.25
  70.1 3.3 convolution_convert_fusion.1
  73.5 4.5 reshape.441
  78.0 6.1 %convolution_convert_fusion.2 = bf16[512,1024]{1,0:T(8,128)(2,1)} fusion(bf16[512,2048]{1,0:T(8,128)(2,1)} %get-tuple-element.128, bf16[2048,1024]{1,0:T(8,128)(2,1)} %param.27), kind=kOutput, calls=%fused_computation.98 | convolution fusion | flops 2148007936 | bytes 7340032 | tf_op jit(solution)/shard_map/dot_general | solution.py:336
  84.1 4.5 reshape.439
  88.6 1.7 collective-permute-start.1
  90.6 6.9 %fusion.149 = (bf16[512,4,1,256]{3,2,1,0:T(2,128)(2,1)}, bf16[512,4,1,256]{3,2,1,0:T(2,128)(2,1)}) fusion(bf16[512,4,2,256]{3,2,1,0:T(2,128)(2,1)} %reshape.439), kind=kLoop, calls=%fused_computation.211 | loop fusion | bytes 4194304 | tf_op jit(solution)/shard_map/slice | solution.py:490
  97.5 4.2 fusion.148
  101.7 6.0 %copy.57 = bf16[512,4,1,256]{0,3,1,2:T(8,128)(2,1)} copy(bf16[512,4,1,256]{3,2,1,0:T(2,128)(2,1)} %get-tuple-element.105) | data formatting | bytes 2097152
  107.6 5.8 %copy.58 = bf16[512,4,1,256]{0,3,1,2:T(8,128)(2,1)} copy(bf16[512,4,1,256]{3,2,1,0:T(2,128)(2,1)} %get-tuple-element.106) | data formatting | bytes 2097152
  113.5 2.3 select_bitcast_fusion.1
  115.8 5.8 %copy.59 = bf16[512,4,1,256]{0,3,1,2:T(8,128)(2,1)} copy(bf16[512,4,1,256]{3,2,1,0:T(2,128)(2,1)} %get-tuple-element.99) | data formatting | bytes 2097152
  121.6 5.8 %copy.60 = bf16[512,4,1,256]{0,3,1,2:T(8,128)(2,1)} copy(bf16[512,4,1,256]{3,2,1,0:T(2,128)(2,1)} %get-tuple-element.100) | data formatting | bytes 2097152
  127.6 3.1 broadcast_select_fusion.7
  132.2 3.3 broadcast_select_fusion.1
  135.9 2.3 multiply_reduce_fusion.1
  138.3 3.8 fusion.145
  143.2 3.1 convolution_convert_fusion.6
  146.4 4.7 %fusion.154 = f32[8,512,512]{1,2,0:T(8,128)} fusion(bf16[512,8,64]{0,2,1:T(8,128)(2,1)S(1)} %bitcast.190, bf16[512,8,64]{0,2,1:T(8,128)(2,1)S(1)} %bitcast.189), kind=kOutput, calls=%fused_computation.214 | convolution fusion | flops 268435456 | bytes 9437184 | tf_op jit(solution)/shard_map/while/body/eval_jaxpr/qhd,khd->hqk/dot_general | solution.py:429
  151.1 2.4 convert_reduce_fusion.3
  154.9 13.5 %fusion.94 = bf16[8,64,512]{2,1,0:T(8,128)(2,1)S(1)} fusion(bf16[512,8,64]{0,2,1:T(8,128)(2,1)} %bitcast.187, f32[8,512,512]{1,2,0:T(8,128)} %fusion.154, f32[8,512,512]{1,2,0:T(8,128)} %copy-done.4, f32[8,512]{1,0:T(8,128)S(1)} %log_add_fusion, pred[512,512]{0,1:T(8,128)(4,1)S(1)} %broadcast_compare_fusion), kind=kOutput, calls=%fused_computation.110 | convolution fusion | flops 291770880 | bytes 18104320 | tf_op jit(solution)/shard_map/while/body/eval_jaxpr/hqk,qhd->khd/dot_general | solution.py:437
  169.3 14.2 %convert_reduce_fusion.4 = (f32[8,64]{1,0:T(8,128)S(1)}, bf16[8,64,512]{2,1,0:T(8,128)(2,1)}) fusion(bf16[512,8,64]{0,2,1:T(8,128)(2,1)S(1)} %bitcast.185, f32[8,512,512]{1,2,0:T(8,128)} %fusion.154, f32[8,512,512]{1,2,0:T(8,128)} %copy-done.4, f32[8,512]{1,0:T(8,128)S(1)} %log_add_fusion, pred[512,512]{0,1:T(8,128)(4,1)S(1)} %broadcast_compare_fusion), kind=kOutput, calls=%fused_computation.131 | convolution fusion | flops 292294656 | bytes 18106368 | tf_op jit(solution)/shard_map/while/body/eval_jaxpr/hqk,khd->qhd/dot_general | solution.py:434
  183.6 2.3 fusion.103
  186.7 1.4 bitcast_select_fusion.3
  188.2 3.7 fusion.73
  193.2 1.9 broadcast_select_fusion.3
  195.2 1.9 add_convert_fusion
  197.1 1.7 collective-permute-start.3
  198.8 1.4 bitcast_select_fusion.1
  200.2 2.3 convert_bitcast_fusion.1
  203.8 1.1 bitcast_select_fusion.9
  205.0 2.3 fusion.99
  210.0 2.1 pad_maximum_fusion
  212.1 6.6 %copy.49 = bf16[7,1024,256]{2,1,0:T(8,128)(2,1)} copy(bf16[7,1024,256]{1,2,0:T(8,128)(2,1)} %pad_maximum_fusion) | data formatting | bytes 7340032 | tf_op jit(solution)/shard_map/concatenate | solution.py:598
  218.8 1.5 broadcast_select_fusion.5
  221.9 1.7 pad_maximum_fusion.1
  223.6 148.3 %group_sum.1 = (bf16[10,2,128,1024]{3,2,1,0:T(8,128)(2,1)}, bf16[14,512,512]{2,1,0:T(8,128)(2,1)}) custom-call(bf16[10,128,1024]{2,1,0:T(8,128)(2,1)} %bitcast.164, bf16[14,512,256]{2,1,0:T(8,128)(2,1)} %bitcast.162), custom_call_target="tpu_custom_call" | custom-call | tf_op jit(solution)/shard_map/group_sum/pallas_call | solution.py:311
  371.9 2.2 slice.111
  374.1 2.5 slice.113
  378.3 2.7 fusion.52
  381.0 1.5 copy.50
  382.4 4.2 copy.52
  386.7 3.6 bitcast_convert_fusion
  390.3 1.2 convert_bitcast_fusion
  391.5 4.4 copy.61
  395.9 62.5 %all-reduce = (f32[1024]{0:T(1024)}, f32[1024]{0:T(1024)}, f32[2,512]{1,0:T(2,128)}, f32[1024]{0:T(1024)}, f32[1024]{0:T(1024)}, /*index=5*/f32[1024]{0:T(1024)}, f32[2048]{0:T(1024)}, f32[1024]{0:T(1024)}) all-reduce(f32[1024]{0:T(1024)S(1)} %get-tuple-element.77, ...), channel_id=1, replica_groups=mesh['dp'=16,'tensor'=2] {'dp'}, use_global_device_ids=true, to_apply=%region_13.14 | all-reduce | flops 9216 | bytes 73728 | tf_op jit(solution)/shard_map/psum | solution.py:623
  458.4 4.0 fusion.51
  (162 shorter events, 21.2 us)
Async XLA Ops:
  0.6 25.3 %copy-start = (bf16[512,1024]{1,0:T(8,128)(2,1)S(1)}, bf16[512,1024]{1,0:T(8,128)(2,1)}, u32[]{:S(2)}) copy-start(bf16[512,1024]{1,0:T(8,128)(2,1)} %param.21) | copy-start | bytes 3145732
  0.7 10.9 %copy-start.22 = (bf16[3,1024,512]{2,1,0:T(8,128)(2,1)S(1)}, bf16[3,1024,512]{2,1,0:T(8,128)(2,1)}, u32[]{:S(2)}) copy-start(bf16[3,1024,512]{2,1,0:T(8,128)(2,1)} %param.19) | copy-start | bytes 9437188
  13.6 4.4 copy-start.32
  15.8 3.7 copy-start.34
  18.0 3.3 copy-start.35
  19.6 3.4 copy-start.4
  25.9 27.0 %copy-start.45 = (f32[1024]{0:T(1024)S(1)}, f32[1024]{0:T(1024)}, u32[]{:S(2)}) copy-start(f32[1024]{0:T(1024)} %param.22) | copy-start | bytes 12292
  26.7 5.5 %copy-start.31 = (bf16[512,1024]{1,0:T(8,128)(2,1)}, bf16[512,1024]{1,0:T(8,128)(2,1)S(1)}, u32[]{:S(2)}) copy-start(bf16[512,1024]{1,0:T(8,128)(2,1)S(1)} %convolution_convert_fusion) | copy-start | bytes 3145732
  26.7 26.3 %collective-permute-start = (bf16[512,1024]{1,0:T(8,128)(2,1)S(1)}, bf16[512,1024]{1,0:T(8,128)(2,1)}, u32[]{:S(2)}, u32[]{:S(2)}) collective-permute-start(bf16[512,1024]{1,0:T(8,128)(2,1)S(1)} %convolution_convert_fusion), channel_id=1, source_target_pairs={{0,1},{1,0},{2,3},{3,2},{4,5},{5,4},{6,7},{7,6},{8,9},{9,8},{10,11... | collective-permute-start | bytes 3145736 | tf_op jit(solution)/shard_map/ppermute | solution.py:470
  29.7 1.6 collective-permute-start.6
  29.8 102.0 %collective-permute-start.11 = (bf16[512,1024]{1,0:T(8,128)(2,1)}, bf16[512,1024]{1,0:T(8,128)(2,1)}, u32[]{:S(2)}, u32[]{:S(2)}) collective-permute-start(bf16[512,1024]{1,0:T(8,128)(2,1)} %fusion.46), channel_id=1, source_target_pairs={{0,2},{2,0},{4,6},{6,4},{8,10},{10,8},{12,14},{14,12},{16,18},{18,... | collective-permute-start | bytes 3145736 | tf_op jit(solution)/shard_map/ppermute | solution.py:476
  30.3 97.2 %collective-permute-start.5 = (bf16[512,1024]{1,0:T(8,128)(2,1)}, bf16[512,1024]{1,0:T(8,128)(2,1)}, u32[]{:S(2)}, u32[]{:S(2)}) collective-permute-start(bf16[512,1024]{1,0:T(8,128)(2,1)} %param.29), channel_id=1, source_target_pairs={{0,2},{2,0},{4,6},{6,4},{8,10},{10,8},{12,14},{14,12},{16,18},{18,... | collective-permute-start | bytes 3145736 | tf_op jit(solution)/shard_map/ppermute | solution.py:476
  32.2 23.6 %copy-start.40 = (f32[1024]{0:T(1024)S(1)}, f32[1024]{0:T(1024)}, u32[]{:S(2)}) copy-start(f32[1024]{0:T(1024)} %param.23) | copy-start | bytes 12292
  32.2 23.6 %copy-start.43 = (f32[1024]{0:T(1024)S(1)}, f32[1024]{0:T(1024)}, u32[]{:S(2)}) copy-start(f32[1024]{0:T(1024)} %param.24) | copy-start | bytes 12292
  55.4 2.6 copy-start.46
  55.4 2.6 copy-start.48
  57.2 6.1 %copy-start.47 = (bf16[2048,1024]{1,0:T(8,128)(2,1)S(1)}, bf16[2048,1024]{1,0:T(8,128)(2,1)}, u32[]{:S(2)}) copy-start(bf16[2048,1024]{1,0:T(8,128)(2,1)} %param.27) | copy-start | bytes 12582916
  57.2 135.4 %collective-permute-start.9 = (bf16[512,1024]{1,0:T(8,128)(2,1)}, bf16[512,1024]{1,0:T(8,128)(2,1)}, u32[]{:S(2)}, u32[]{:S(2)}) collective-permute-start(bf16[512,1024]{1,0:T(8,128)(2,1)} %add_convert_fusion.2), channel_id=1, source_target_pairs={{0,2},{2,0},{4,6},{6,4},{8,10},{10,8},{12,14},{14,12},{16,18},{18,... | collective-permute-start | bytes 3145736 | tf_op jit(solution)/shard_map/ppermute | solution.py:476
  68.8 1.3 copy-start.25
  88.6 8.9 %copy-start.7 = (bf16[512,4,2,256]{3,2,1,0:T(2,128)(2,1)S(1)}, bf16[512,4,2,256]{3,2,1,0:T(2,128)(2,1)}, u32[]{:S(2)}) copy-start(bf16[512,4,2,256]{3,2,1,0:T(2,128)(2,1)} %reshape.441) | copy-start | bytes 6291460
  88.6 49.7 %collective-permute-start.1 = (bf16[512,1024]{1,0:T(8,128)(2,1)}, bf16[512,1024]{1,0:T(8,128)(2,1)}, u32[]{:S(2)}, u32[]{:S(2)}) collective-permute-start(bf16[512,1024]{1,0:T(8,128)(2,1)} %convolution_convert_fusion.2), channel_id=1, source_target_pairs={{0,1},{1,0},{2,3},{3,2},{4,5},{5,4},{6,7},{7,6},{8,9},{9,8},{10,11... | collective-permute-start | bytes 3145736 | tf_op jit(solution)/shard_map/ppermute | solution.py:470
  90.3 45.6 %collective-permute-start.2 = (bf16[512,1024]{1,0:T(8,128)(2,1)}, bf16[512,1024]{1,0:T(8,128)(2,1)}, u32[]{:S(2)}, u32[]{:S(2)}) collective-permute-start(bf16[512,1024]{1,0:T(8,128)(2,1)} %convolution_convert_fusion.1), channel_id=1, source_target_pairs={{0,1},{1,0},{2,3},{3,2},{4,5},{5,4},{6,7},{7,6},{8,9},{9,8},{10,11... | collective-permute-start | bytes 3145736 | tf_op jit(solution)/shard_map/ppermute | solution.py:470
  127.4 3.3 copy-start.8
  127.4 3.3 copy-start.10
  127.4 4.7 %copy-start.2 = (bf16[512,1024]{1,0:T(8,128)(2,1)S(1)}, bf16[512,1024]{1,0:T(8,128)(2,1)}, u32[]{:S(2)}) copy-start(bf16[512,1024]{1,0:T(8,128)(2,1)} %param.15) | copy-start | bytes 3145732
  127.4 4.7 %copy-start.41 = (f32[1024]{0:T(1024)S(1)}, f32[1024]{0:T(1024)}, u32[]{:S(2)}) copy-start(f32[1024]{0:T(1024)} %param.17) | copy-start | bytes 12292
  127.4 4.7 %copy-start.42 = (f32[1024]{0:T(1024)S(1)}, f32[1024]{0:T(1024)}, u32[]{:S(2)}) copy-start(f32[1024]{0:T(1024)} %param.18) | copy-start | bytes 12292
  127.5 59.2 %collective-permute-start.4 = (bf16[512,4,256]{0,2,1:T(8,128)(2,1)}, bf16[512,4,256]{0,2,1:T(8,128)(2,1)}, u32[]{:S(2)}, u32[]{:S(2)}) collective-permute-start(bf16[512,4,256]{0,2,1:T(8,128)(2,1)} %select_bitcast_fusion.1), channel_id=1, source_target_pairs={{0,2},{2,0},{4,6},{6,4},{8,10},{10,8},{12,14},{14,12},{16,18},{18,... | collective-permute-start | bytes 3145736 | tf_op jit(solution)/shard_map/ppermute | solution.py:476
  130.7 5.2 %copy-start.21 = (bf16[512,1024]{1,0:T(8,128)(2,1)S(1)}, bf16[512,1024]{1,0:T(8,128)(2,1)}, u32[]{:S(2)}) copy-start(bf16[512,1024]{1,0:T(8,128)(2,1)} %convolution_convert_fusion.1) | copy-start | bytes 3145732
  131.8 65.2 %collective-permute-start.8 = (bf16[512,4,256]{0,2,1:T(8,128)(2,1)}, bf16[512,4,256]{0,2,1:T(8,128)(2,1)}, u32[]{:S(2)}, u32[]{:S(2)}) collective-permute-start(bf16[512,4,256]{0,2,1:T(8,128)(2,1)} %select_bitcast_fusion), channel_id=1, source_target_pairs={{0,2},{2,0},{4,6},{6,4},{8,10},{10,8},{12,14},{14,12},{16,18},{18,... | collective-permute-start | bytes 3145736 | tf_op jit(solution)/shard_map/ppermute | solution.py:476
  135.5 2.8 copy-start.30
  135.5 2.8 copy-start.44
  142.1 4.2 copy-start.5
  142.1 4.3 copy-start.36
  142.1 9.0 %slice-start = ((s8[8388608]{0:T(1024)(128)(4,1)}), s8[4194304]{0:T(1024)(128)(4,1)S(1)}, s32[]{:S(2)}) async-start(s8[8388608]{0:T(1024)(128)(4,1)} %bitcast.159), calls=%async_computation | async-start | bytes 8388608
  146.3 72.5 %collective-permute-start.7 = (bf16[512,1024]{1,0:T(8,128)(2,1)}, bf16[512,1024]{1,0:T(8,128)(2,1)}, u32[]{:S(2)}, u32[]{:S(2)}) collective-permute-start(bf16[512,1024]{1,0:T(8,128)(2,1)} %convert_element_type.247), channel_id=1, source_target_pairs={{0,2},{2,0},{4,6},{6,4},{8,10},{10,8},{12,14},{14,12},{16,18},{18,... | collective-permute-start | bytes 3145736 | tf_op jit(solution)/shard_map/ppermute | solution.py:476
  146.4 4.7 %slice-start.1 = ((s8[8388608]{0:T(1024)(128)(4,1)}), s8[4194304]{0:T(1024)(128)(4,1)S(1)}, s32[]{:S(2)}) async-start(s8[8388608]{0:T(1024)(128)(4,1)} %bitcast.159), calls=%async_computation.1 | async-start | bytes 8388608
  154.4 14.9 %copy-start.33 = (bf16[512,512]{0,1:T(8,128)(2,1)S(1)}, bf16[512,512]{0,1:T(8,128)(2,1)}, u32[]{:S(2)}) copy-start(bf16[512,512]{0,1:T(8,128)(2,1)} %copy-done.32) | copy-start | bytes 1572868
  154.4 48.3 %collective-permute-start.13 = (bf16[512,1,256]{0,2,1:T(8,128)(2,1)}, bf16[512,1,256]{0,2,1:T(8,128)(2,1)}, u32[]{:S(2)}, u32[]{:S(2)}) collective-permute-start(bf16[512,1,256]{0,2,1:T(8,128)(2,1)} %select_bitcast_fusion.2), channel_id=1, source_target_pairs={{0,2},{2,0},{4,6},{6,4},{8,10},{10,8},{12,14},{14,12},{16,18},{18,... | collective-permute-start | bytes 786440 | tf_op jit(solution)/shard_map/ppermute | solution.py:476
  183.6 2.3 copy-start.16
  183.6 3.1 copy-start.12
  183.6 3.1 copy-start.13
  185.9 2.3 copy-start.28
  185.9 2.3 copy-start.29
  186.6 17.1 %collective-permute-start.10 = (bf16[512,1,256]{0,2,1:T(8,128)(2,1)}, bf16[512,1,256]{0,2,1:T(8,128)(2,1)}, u32[]{:S(2)}, u32[]{:S(2)}) collective-permute-start(bf16[512,1,256]{0,2,1:T(8,128)(2,1)} %select_bitcast_fusion.4), channel_id=1, source_target_pairs={{0,2},{2,0},{4,6},{6,4},{8,10},{10,8},{12,14},{14,12},{16,18},{18,... | collective-permute-start | bytes 786440 | tf_op jit(solution)/shard_map/ppermute | solution.py:476
  188.2 3.7 copy-start.23
  192.6 2.5 copy-start.19
  192.8 15.2 %collective-permute-start.12 = (bf16[512,1,256]{0,2,1:T(8,128)(2,1)S(1)}, bf16[512,1,256]{0,2,1:T(8,128)(2,1)}, u32[]{:S(2)}, u32[]{:S(2)}) collective-permute-start(bf16[512,1,256]{0,2,1:T(8,128)(2,1)S(1)} %copy-done.39), channel_id=1, source_target_pairs={{0,2},{2,0},{4,6},{6,4},{8,10},{10,8},{12,14},{14,12},{16,18},{18,... | collective-permute-start | bytes 786440 | tf_op jit(solution)/shard_map/ppermute | solution.py:476
  195.1 3.7 copy-start.9
  195.2 3.6 copy-start.11
  197.1 181.1 %collective-permute-start.3 = (bf16[512,1024]{1,0:T(8,128)(2,1)}, bf16[512,1024]{1,0:T(8,128)(2,1)}, u32[]{:S(2)}, u32[]{:S(2)}) collective-permute-start(bf16[512,1024]{1,0:T(8,128)(2,1)} %add_convert_fusion), channel_id=1, source_target_pairs={{0,1},{1,0},{2,3},{3,2},{4,5},{5,4},{6,7},{7,6},{8,9},{9,8},{10,11... | collective-permute-start | bytes 3145736 | tf_op jit(solution)/shard_map/ppermute | solution.py:470
  200.2 2.5 copy-start.20
  200.2 3.6 copy-start.17
  203.8 3.5 copy-start.26
  203.8 3.5 copy-start.27
  207.3 1.0 copy-start.15
  212.1 6.7 %copy-start.6 = (f32[512,1024]{1,0:T(8,128)S(1)}, f32[512,1024]{1,0:T(8,128)}, u32[]{:S(2)}) copy-start(f32[512,1024]{1,0:T(8,128)} %copy-done.5) | copy-start | bytes 6291460
  218.8 1.5 copy-start.37
  218.8 1.5 copy-start.38
  220.3 1.6 copy-start.24
  371.9 4.8 %slice-start.2 = ((s8[5242880]{0:T(1024)(128)(4,1)}), s8[4194304]{0:T(1024)(128)(4,1)S(1)}, s32[]{:S(2)}) async-start(s8[5242880]{0:T(1024)(128)(4,1)} %bitcast.167), calls=%async_computation.2 | async-start | bytes 8388608
  374.1 2.7 slice-start.3
  377.1 1.2 copy-start.3
  395.9 66.5 %copy-start.1 = (bf16[512,1024]{1,0:T(8,128)(2,1)S(1)}, bf16[512,1024]{1,0:T(8,128)(2,1)}, u32[]{:S(2)}) copy-start(bf16[512,1024]{1,0:T(8,128)(2,1)} %param.21) | copy-start | bytes 3145732
  (3 other events, 2.8 us)

commit v2 on v1

v2 whole, which is shorter than its diff:
```python
import jax
import jax.numpy as jnp
from jax import lax
from jax.experimental import pallas as pl
from jax.experimental.pallas import tpu as pltpu
from jax.sharding import PartitionSpec as P

MESH = pl.DeviceIdType.MESH
bf16, f32 = jnp.bfloat16, jnp.float32
CELL = 16
STAGES = 6


def place():
    at = lax.axis_index("dp")
    base = (at // CELL) * CELL
    inner = at - base
    z = inner // 4
    y = (inner // 2) % 2
    core = inner % 2
    return base, z, y, core


class Summer:
    def __init__(self, loc_a, loc_b, bufs, out_a, out_b, sems):
        self.loc_a, self.loc_b = loc_a, loc_b
        (self.a1, self.a2, self.a3, self.b1, self.b2, self.b3) = bufs
        self.out_a, self.out_b = out_a, out_b
        self.as_, self.ar_, self.bs_, self.br_, self.ls_ = sems
        self.na = loc_a.shape[0]
        self.nb = loc_b.shape[0]
        self.ha = loc_a.shape[1] // 2
        self.hb = loc_b.shape[1] // 2
        base, z, y, core = place()
        self.y, self.core = y, core
        self.outer = jnp.logical_or(z == 0, z == 3)
        self.mid = jnp.logical_not(self.outer)
        self.mine = jnp.where(z >= 2, 1, 0)
        across = 3 - z
        toward = jnp.where(z < 2, 1 - z, 5 - z)
        tensor = lax.axis_index("tensor")

        def dev(zz, yy, cc):
            return (base + zz * 4 + yy * 2 + cc, tensor)

        self.to_sib = dev(z, y, 1 - core)
        self.to_y = dev(z, 1 - y, core)
        self.to_mid = dev(across, y, core)
        self.to_z = dev(toward, y, core)

    def la(self, i, h):
        return self.loc_a.at[i, pl.ds(pl.multiple_of(h * self.ha, self.ha), self.ha), :]

    def lb(self, i, h):
        return self.loc_b.at[i, pl.ds(pl.multiple_of(h * self.hb, self.hb), self.hb), :]

    def oa(self, i, h, core):
        at = lax.rem(i, 2) * 2 * self.ha + h * self.ha
        return self.out_a.at[i // 2, core, pl.ds(pl.multiple_of(at, self.ha), self.ha), :]

    def ob(self, i, h, core):
        w = self.loc_b.shape[2]
        at = lax.rem(i, 2) * 2 * self.hb + h * self.hb
        return self.out_b.at[
            i // 2,
            pl.ds(pl.multiple_of(at, self.hb), self.hb),
            pl.ds(pl.multiple_of(core * w, w), w),
        ]

    def ca(self, i, kind, recv, src, dst, to):
        return pltpu.make_async_remote_copy(
            src, dst, self.as_.at[i, kind], self.ar_.at[i, recv], device_id=to, device_id_type=MESH
        )

    def cb(self, i, kind, recv, src, dst, to):
        return pltpu.make_async_remote_copy(
            src, dst, self.bs_.at[i, kind], self.br_.at[i, recv], device_id=to, device_id_type=MESH
        )

    def a_y(self, i):
        return self.ca(i, 0, 0, self.la(i, 1 - self.y), self.a1.at[i], self.to_y)

    def a_in(self, i):
        return self.ca(i, 1, 1, self.la(i, self.y), self.a2.at[i], self.to_z)

    def a_mid(self, i):
        return self.ca(i, 1, 2, self.la(i, self.y), self.a3.at[i], self.to_mid)

    def a_out(self, i):
        return self.ca(i, 2, 3, self.a2.at[i], self.oa(i, self.y, self.core), self.to_z)

    def a_done(self, i, kind, recv, src, to):
        return self.ca(i, kind, recv, src, self.oa(i, self.y, self.core), to)

    def a_keep(self, i):
        return pltpu.make_async_copy(self.a2.at[i], self.oa(i, self.y, self.core), self.ls_.at[0, i])

    def a_fwd(self, i):
        o = self.oa(i, 1 - self.y, self.core)
        return self.ca(i, 5, 6, o, o, self.to_sib)

    def step_a(self, i, stage):
        y = self.y
        if stage == 0:
            self.a_y(i).start()
        elif stage == 1:
            self.a_y(i).wait_recv()
            v = self.la(i, y)
            v[...] = (v[...].astype(f32) + self.a1[i].astype(f32)).astype(bf16)

            @pl.when(self.outer)
            def _():
                self.a_in(i).start()
        elif stage == 2:
            @pl.when(self.mid)
            def _():
                self.a_in(i).wait_recv()
                v = self.la(i, y)
                v[...] = (v[...].astype(f32) + self.a2[i].astype(f32)).astype(bf16)
                self.a_mid(i).start()
        elif stage == 3:
            @pl.when(self.mid)
            def _():
                self.a_mid(i).wait_recv()
                self.a2[i] = (self.la(i, y)[...].astype(f32) + self.a3[i].astype(f32)).astype(bf16)
                self.a_out(i).start()
                src = self.a2.at[i]
                self.a_done(i, 3, 4, src, self.to_y).start()
                self.a_done(i, 4, 5, src, self.to_sib).start()
                self.a_keep(i).start()
        elif stage == 4:
            @pl.when(self.outer)
            def _():
                self.a_out(i).wait_recv()
                src = self.oa(i, y, self.core)
                self.a_done(i, 3, 4, src, self.to_y).start()
                self.a_done(i, 4, 5, src, self.to_sib).start()
        elif stage == 5:
            self.a_done(i, 3, 4, self.oa(i, y, self.core), self.to_y).wait_recv()
            self.a_fwd(i).start()

    def end_a(self, i):
        src = self.a2.at[i]
        self.a_y(i).wait_send()
        self.a_in(i).wait_send()

        @pl.when(self.mid)
        def _():
            self.a_out(i).wait_send()
            self.a_keep(i).wait()

        self.a_done(i, 3, 4, src, self.to_y).wait_send()
        self.a_done(i, 4, 5, src, self.to_sib).wait_send()
        self.a_fwd(i).wait_send()
        self.a_done(i, 4, 5, src, self.to_sib).wait_recv()
        self.a_fwd(i).wait_recv()

    def b_in(self, i):
        return self.cb(i, 0, 0, self.loc_b.at[i], self.b1.at[i], self.to_z)

    def b_mid(self, i):
        return self.cb(i, 0, 1, self.lb(i, 1 - self.mine), self.b2.at[i], self.to_mid)

    def b_y(self, i):
        return self.cb(i, 1, 2, self.lb(i, self.mine), self.b3.at[i], self.to_y)

    def fin_b(self, i):
        return self.b1.at[i, pl.ds(0, self.hb), :]

    def b_done(self, i, kind, recv, src, h, to):
        return self.cb(i, kind, recv, src, self.ob(i, h, self.core), to)

    def b_keep(self, i):
        return pltpu.make_async_copy(
            self.fin_b(i), self.ob(i, self.mine, self.core), self.ls_.at[1, i]
        )

    def step_b(self, i, stage):
        mine, core = self.mine, self.core
        if stage == 0:
            @pl.when(self.outer)
            def _():
                self.b_in(i).start()
        elif stage == 1:
            @pl.when(self.mid)
            def _():
                self.b_in(i).wait_recv()
                self.loc_b[i] = (self.loc_b[i].astype(f32) + self.b1[i].astype(f32)).astype(bf16)
                self.b_mid(i).start()
        elif stage == 2:
            @pl.when(self.mid)
            def _():
                self.b_mid(i).wait_recv()
                v = self.lb(i, mine)
                v[...] = (v[...].astype(f32) + self.b2[i].astype(f32)).astype(bf16)
                self.b_y(i).start()
        elif stage == 3:
            @pl.when(self.mid)
            def _():
                self.b_y(i).wait_recv()
                fin = self.fin_b(i)
                fin[...] = (self.lb(i, mine)[...].astype(f32) + self.b3[i].astype(f32)).astype(bf16)
                self.b_done(i, 2, 4, fin, mine, self.to_mid).start()
                self.b_done(i, 3, 3, fin, mine, self.to_z).start()
                self.b_done(i, 4, 5, fin, mine, self.to_sib).start()
                self.b_keep(i).start()
        elif stage == 4:
            @pl.when(self.mid)
            def _():
                o = self.ob(i, 1 - mine, core)
                self.b_done(i, 2, 4, o, 1 - mine, self.to_mid).wait_recv()
                self.b_done(i, 5, 4, o, 1 - mine, self.to_z).start()
                self.b_done(i, 6, 6, o, 1 - mine, self.to_sib).start()

            @pl.when(self.outer)
            def _():
                o = self.ob(i, mine, core)
                self.b_done(i, 3, 3, o, mine, self.to_z).wait_recv()
                self.b_done(i, 4, 5, o, mine, self.to_sib).start()
        elif stage == 5:
            @pl.when(self.outer)
            def _():
                o = self.ob(i, 1 - mine, core)
                self.b_done(i, 5, 4, o, 1 - mine, self.to_z).wait_recv()
                self.b_done(i, 6, 6, o, 1 - mine, self.to_sib).start()

    def end_b(self, i):
        fin = self.fin_b(i)
        mine = self.mine

        @pl.when(self.outer)
        def _():
            self.b_in(i).wait_send()

        @pl.when(self.mid)
        def _():
            self.b_mid(i).wait_send()
            self.b_y(i).wait_send()
            self.b_done(i, 2, 4, fin, mine, self.to_mid).wait_send()
            self.b_done(i, 3, 3, fin, mine, self.to_z).wait_send()
            self.b_done(i, 5, 4, fin, mine, self.to_z).wait_send()
            self.b_keep(i).wait()

        self.b_done(i, 4, 5, fin, mine, self.to_sib).wait_send()
        self.b_done(i, 6, 6, fin, mine, self.to_sib).wait_send()
        self.b_done(i, 4, 5, fin, mine, self.to_sib).wait_recv()
        self.b_done(i, 6, 6, fin, mine, self.to_sib).wait_recv()

    def step(self, t):
        for stage in range(STAGES):
            i = t - stage

            @pl.when(jnp.logical_and(i >= 0, i < self.na))
            def _():
                self.step_a(i, stage)

            @pl.when(jnp.logical_and(i >= 0, i < self.nb))
            def _():
                self.step_b(i, stage)

    def steps(self, lo, hi):
        def body(t, _):
            self.step(t)
            return 0

        lax.fori_loop(lo, hi, body, 0)

    def end(self):
        def body_a(i, _):
            self.end_a(i)
            return 0

        def body_b(i, _):
            self.end_b(i)
            return 0

        lax.fori_loop(0, self.na, body_a, 0)
        lax.fori_loop(0, self.nb, body_b, 0)


def scratch_of(na, ra, wa, nb, rb, wb):
    return [
        pltpu.VMEM((na, ra // 2, wa), bf16),
        pltpu.VMEM((na, ra // 2, wa), bf16),
        pltpu.VMEM((na, ra // 2, wa), bf16),
        pltpu.VMEM((nb, rb, wb), bf16),
        pltpu.VMEM((nb, rb // 2, wb), bf16),
        pltpu.VMEM((nb, rb // 2, wb), bf16),
        pltpu.SemaphoreType.DMA((na, 6)),
        pltpu.SemaphoreType.DMA((na, 7)),
        pltpu.SemaphoreType.DMA((nb, 7)),
        pltpu.SemaphoreType.DMA((nb, 7)),
        pltpu.SemaphoreType.DMA((2, max(na, nb))),
    ]


def split_rows(value):
    rows, cols = value.shape
    return jnp.sum(value.reshape(rows // 8, 8, cols), axis=0)


def erf(value):
    x = jnp.clip(value, -4.0, 4.0)
    x2 = x * x
    top = -2.72614225801306e-10
    for c in (
        2.77068142495902e-08,
        -2.10102402082508e-06,
        -5.69250639462346e-05,
        -7.34990630326855e-04,
        -2.95459980854025e-03,
        -1.60960333262415e-02,
    ):
        top = top * x2 + c
    low = -1.45660718464996e-05
    for c in (
        -2.13374055278905e-04,
        -1.68282697438203e-03,
        -7.37332916720468e-03,
        -1.42647390514189e-02,
    ):
        low = low * x2 + c
    return x * top / low


def gelu_parts(u):
    cdf = 0.5 * (1.0 + erf(u * 0.7071067811865476))
    pdf = jnp.exp(-0.5 * u * u) * 0.3989422804014327
    return u * cdf, cdf + u * pdf


def normed(rows_in):
    centred = rows_in - jnp.mean(rows_in, axis=-1, keepdims=True)
    scale = lax.rsqrt(jnp.mean(centred * centred, axis=-1, keepdims=True) + 1e-06)
    return centred * scale, scale


def mm(left, right):
    return jnp.dot(left, right, preferred_element_type=f32)


def mm_tn(left, right):
    return lax.dot_general(left, right, (((0,), (0,)), ((), ())), preferred_element_type=f32)


def mm_nt(left, right):
    return lax.dot_general(left, right, (((1,), (1,)), ((), ())), preferred_element_type=f32)


LINKS = {
    "w": 4, "c": 1, "o": 4, "osib": 2, "h2t": 4, "act": 4, "pre": 4, "x0": 4, "x1": 4, "x2": 4,
    "dyb": 1, "h1t": 1, "dqkv": 6, "small": 5,
}
LINK_AT = {}
for _name, _count in LINKS.items():
    LINK_AT[_name] = sum(LINKS[n] for n in LINK_AT)
N_LINKS = sum(LINKS.values())


def layer_kernel(
    clip, again, ashift, qvb, outb, mgain, mshift, upb, downb,
    tok_h, wqkv_h, wout_h, wup_h, wdown_h, cot_h,
    lo_h, gt_h, out_a, out_b, small_h,
    tok, wqkv, wout, wup, wdown, cpair, hid, h1t, q, k, v, o_own, o_peer, o_sib, y1, h2t,
    act, pre, act_sib, pre_sib, xs0, xs1, xr0, xr1, dy1, dob, scr0, scr1, small, small_r, sums,
    loc_a, loc_b, a1, a2, a3, b1, b2, b3,
    as_, ar_, bs_, br_, ls_, lsem, ssem, rsem,
):
    rows = tok.shape[0]
    width = tok.shape[1]
    sm = Summer(loc_a, loc_b, (a1, a2, a3, b1, b2, b3), out_a, out_b, (as_, ar_, bs_, br_, ls_))
    base, z, y, core = place()
    t = lax.axis_index("tensor")
    to_x = (lax.axis_index("dp"), 1 - t)
    to_sib, to_y = sm.to_sib, sm.to_y

    def rc(name, i, src, dst, to):
        at = LINK_AT[name] + i
        return pltpu.make_async_remote_copy(
            src, dst, ssem.at[at], rsem.at[at], device_id=to, device_id_type=MESH
        )

    def cols(i, n=128):
        return pl.ds(pl.multiple_of(i * n, n), n)

    def loop(n, body):
        def wrapped(i, _):
            body(i)
            return 0

        lax.fori_loop(0, n, wrapped, 0)

    def load(i, src, dst):
        return pltpu.make_async_copy(src, dst, lsem.at[i])

    loads = [
        load(0, tok_h, tok),
        load(1, wqkv_h, wqkv),
        load(2, wout_h, wout.at[t]),
        load(3, wup_h, wup),
        load(4, cot_h, cpair.at[0]),
        load(5, wdown_h, wdown),
    ]
    quarter = 2 * y + core
    part = wout_h.shape[0] // 4

    def rows_of(i):
        return pl.ds(pl.multiple_of(i * part, part), part)

    def w_at(i):
        return wout.at[1 - t, rows_of(i), :]

    w_out = rc("w", 0, wout_h.at[rows_of(quarter), :], wout.at[t, rows_of(quarter), :], to_x)
    w_in = rc("w", 0, wout_h.at[rows_of(quarter), :], w_at(quarter), to_x)
    w_y = rc("w", 1, w_at(quarter), w_at(quarter), to_y)
    w_s0 = rc("w", 2, w_at(quarter), w_at(quarter), to_sib)
    other = 2 * (1 - y) + core
    w_s1 = rc("w", 3, w_at(other), w_at(other), to_sib)
    c_out = rc("c", 0, cot_h, cpair.at[1], to_sib)
    loads[0].start()
    loads[1].start()
    w_out.start()
    for item in loads[2:]:
        item.start()
    c_out.start()

    loads[0].wait()
    tile = 64

    def norm_one(i):
        r = pl.ds(pl.multiple_of(i * tile, tile), tile)
        n1, _ = normed(tok[r, :].astype(f32))
        hid[r, :] = (n1 * again[...] + ashift[...]).astype(bf16)

    loop(rows // tile, norm_one)
    loads[1].wait()
    heads_w = q.shape[1]
    lane = lax.broadcasted_iota(jnp.int32, (1, 128), 1)

    def half_of(value, e):
        keep = (lane < 64) if e == 0 else (lane >= 64)
        return jnp.where(keep, value.astype(f32), 0.0).astype(bf16)

    end0 = clip[0, 0]
    end1 = end0 + clip[0, 1]
    end2 = end1 + clip[0, 2]

    def seg_of(index):
        one = lambda e: (index >= e).astype(jnp.int32)
        return one(end0) + one(end1) + one(end2)

    key_seg = seg_of(lax.broadcasted_iota(jnp.int32, (1, rows), 1))
    sub = 32

    def softmax_rows(i):
        r = pl.ds(pl.multiple_of(i * sub, sub), sub)
        row_seg = seg_of(lax.broadcasted_iota(jnp.int32, (sub, 1), 0) + i * sub)
        s = jnp.where(row_seg == key_seg, scr0[r, :], -1e30)
        w = jnp.exp(s - jnp.max(s, axis=1, keepdims=True))
        return r, w * (1.0 / jnp.sum(w, axis=1, keepdims=True))

    def make_qkv(g):
        c4 = cols(g, 256)
        h = hid[...]
        q[:, c4] = ((mm(h, wqkv[0, :, c4]) + qvb[pl.ds(0, 1), c4]).astype(bf16) * 0.125).astype(bf16)
        k[:, c4] = mm(h, wqkv[1, :, c4]).astype(bf16)
        v[:, c4] = (mm(h, wqkv[2, :, c4]) + qvb[pl.ds(1, 1), c4]).astype(bf16)

    def o_send(pr):
        return rc("o", pr, o_own.at[:, cols(pr)], o_peer.at[:, cols(pr)], to_x)

    def osib_send(pr):
        m = lax.rem(pr, 2)
        return rc("osib", m, o_own.at[:, cols(pr)], o_sib.at[:, cols(m)], to_sib)

    def attend(pr):
        c2 = cols(pr)
        total = None
        for e in range(2):
            scr0[...] = mm_nt(half_of(q[:, c2], e), k[:, c2])

            def soft(i):
                r, p = softmax_rows(i)
                xs0[r, pl.ds(0, rows)] = p.astype(bf16)

            loop(rows // sub, soft)
            term = mm(xs0[:, pl.ds(0, rows)], half_of(v[:, c2], e))
            total = term if total is None else total + term
        o_own[:, c2] = total.astype(bf16)
        o_send(pr).start()

        @pl.when(pr // 2 == 1 - core)
        def _():
            osib_send(pr).start()

    def group_of_heads(g):
        make_qkv(g)
        attend(2 * g)
        attend(2 * g + 1)

    loop(heads_w // 256, group_of_heads)

    w_in.wait_recv()
    w_y.start()
    w_s0.start()
    loads[2].wait()
    nrow = 128

    def own_part(i):
        r = pl.ds(pl.multiple_of(i * nrow, nrow), nrow)
        y1[r, :] = mm(o_own[r, :], wout[t])

    loop(rows // nrow, own_part)
    w_y.wait_recv()
    w_s1.start()
    w_s0.wait_recv()
    w_s1.wait_recv()
    w_y.wait_send()
    w_s0.wait_send()
    w_s1.wait_send()
    for pr in range(4):
        o_send(pr).wait_recv()

    def h2t_send(i):
        return rc("h2t", i, h2t.at[0, :, cols(i, nrow)], h2t.at[1, :, cols(i, nrow)], to_sib)

    def norm_two(i):
        r = pl.ds(pl.multiple_of(i * nrow, nrow), nrow)
        x = tok[r, :].astype(f32)
        y = x + (y1[r, :] + mm(o_peer[r, :], wout[1 - t])) + outb[...]
        y1[r, :] = y
        n2, _ = normed(y)
        h2 = (n2 * mgain[...] + mshift[...]).astype(bf16)
        hid_two[r, :] = h2
        h2t[0, :, cols(i, nrow)] = h2.T
        h2t_send(i).start()

    hid_two = xs1
    loop(rows // nrow, norm_two)

    loads[3].wait()
    loads[4].wait()
    loads[5].wait()
    c_out.wait_recv()

    def act_send(j):
        c4 = cols(2 * j + 1 - core, 256)
        return rc("act", j, act.at[:, c4], act_sib.at[j], to_sib)

    def pre_send(j):
        c4 = cols(2 * j + 1 - core, 256)
        return rc("pre", j, pre.at[:, c4], pre_sib.at[j], to_sib)

    def hidden(piece):
        c4 = cols(piece, 256)
        half = pl.ds(0, 256)
        scr0[:, half] = mm(hid_two[...], wup[:, c4]) + upb[:, c4]
        scr1[:, half] = mm_nt(cpair[0], wdown[c4, :])

        def slope(i, total):
            r = pl.ds(pl.multiple_of(i * tile, tile), tile)
            a, d = gelu_parts(scr0[r, half])
            du = (scr1[r, half] * d).astype(bf16)
            act[r, c4] = a.astype(bf16)
            pre[r, c4] = du
            return total + split_rows(du.astype(f32))

        total = lax.fori_loop(0, rows // tile, slope, jnp.zeros((8, 256), f32))
        row = 6 + piece // 4
        small[pl.ds(row, 1), cols(lax.rem(piece, 4), 256)] = jnp.sum(total, axis=0, keepdims=True)

    def chunk(j):
        hidden(2 * j + 1 - core)
        act_send(j).start()
        pre_send(j).start()
        hidden(2 * j + core)
        mine = cols(2 * j + core, 256)
        act_send(j).wait_recv()
        for n in range(width // 512):
            wide = pl.ds(n * 512, 512)
            block = mm_tn(act[:, mine], cpair[0, :, wide]) + mm_tn(act_sib[j], cpair[1, :, wide])
            low = block.astype(bf16)
            loc_a[2 * j, :, wide] = low[:128]
            loc_a[2 * j + 1, :, wide] = low[128:]
        pre_send(j).wait_recv()
        for m in range(2):
            high = pl.ds(m * 512, 512)
            loc_b[2 * j + m] = (
                mm(h2t[0, high, :], pre[:, mine]) + mm(h2t[1, high, :], pre_sib[j])
            ).astype(bf16)

    def first_wait():
        for i in range(4):
            h2t_send(i).wait_recv()

    first_wait()
    chunk(0)
    sm.step(0)
    chunk(1)
    chunk(2)
    sm.step(1)
    chunk(3)

    def x_send(name, n, src, dst):
        return rc(name, n, src.at[:, cols(n, 256)], dst.at[:, cols(n, 256)], to_x)

    def back_two(n):
        xs0[:, cols(n, 256)] = mm_nt(pre[...], wup[cols(n, 256), :]).astype(bf16)
        x_send("x0", n, xs0, xr0).start()

    loop(width // 256, back_two)
    sm.step(2)

    def forward_two(n):
        xs1[:, cols(n, 256)] = mm(act[...], wdown[:, cols(n, 256)]).astype(bf16)
        x_send("x1", n, xs1, xr1).start()

    loop(width // 256, forward_two)

    def turn_first(i):
        r = pl.ds(pl.multiple_of(i * nrow, nrow), nrow)
        h1t[0, :, cols(i, nrow)] = hid[r, :].T

    loop(rows // nrow, turn_first)
    h1t_out = rc("h1t", 0, h1t.at[0], h1t.at[1], to_sib)
    h1t_out.start()

    def cot_sum(i, total):
        r = pl.ds(pl.multiple_of(i * tile, tile), tile)
        return total + split_rows(cpair[0, r, :].astype(f32))

    total = lax.fori_loop(0, rows // tile, cot_sum, jnp.zeros((8, width), f32))
    small[pl.ds(8, 1), :] = jnp.sum(total, axis=0, keepdims=True)
    sm.step(3)
    sm.step(4)

    for n in range(4):
        x_send("x0", n, xs0, xr0).wait_recv()
    sums[...] = jnp.zeros_like(sums)
    back = 32
    dyb = xr0

    def norm_two_back(i):
        r = pl.ds(pl.multiple_of(i * back, back), back)
        g = xs0[r, :].astype(f32) + xr0[r, :].astype(f32)
        n2, r2 = normed(y1[r, :])
        gn = g * n2
        sums[0] += split_rows(gn)
        sums[1] += split_rows(g)
        e2 = g * mgain[...]
        m1 = jnp.mean(e2, axis=-1, keepdims=True)
        m2 = jnp.mean(e2 * n2, axis=-1, keepdims=True)
        d = cpair[0, r, :].astype(f32) + r2 * (e2 - m1 - n2 * m2)
        sums[2] += split_rows(d)
        dy1[r, :] = d
        dyb[r, :] = d.astype(bf16)

    loop(rows // back, norm_two_back)
    dyb_out = rc("dyb", 0, dyb, wout.at[1 - t], to_sib)
    dyb_out.start()
    for i, row in enumerate((4, 5, 3)):
        small[pl.ds(row, 1), :] = jnp.sum(sums[i], axis=0, keepdims=True)
    for n in range(4):
        x_send("x0", n, xs0, xr0).wait_send()

    def back_heads(n):
        dob[:, cols(n, 256)] = mm_nt(dyb[...], wout[t, cols(n, 256), :]).astype(bf16)

    loop(heads_w // 256, back_heads)
    sm.step(5)
    osib_send(0).wait_recv()
    osib_send(1).wait_recv()
    dyb_out.wait_recv()
    for n in range(width // 512):
        wide = pl.ds(n * 512, 512)
        low = (
            mm_tn(o_own[:, cols(core, 256)], dyb[:, wide]) + mm_tn(o_sib[...], wout[1 - t, :, wide])
        ).astype(bf16)
        loc_a[8, :, wide] = low[:128]
        loc_a[9, :, wide] = low[128:]

    def dqkv_send(w, m, src, pr):
        return rc("dqkv", 2 * w + m, src.at[:, cols(pr)], act_sib.at[w, :, cols(m)], to_sib)

    def attend_back(pr):
        c2 = cols(pr)
        p_at, ds_at = pl.ds(0, rows), pl.ds(rows, rows)
        dq = dk = dv = None
        for e in range(2):
            q_e, do_e = half_of(q[:, c2], e), half_of(dob[:, c2], e)
            scr0[...] = mm_nt(q_e, k[:, c2])
            scr1[...] = mm_nt(do_e, v[:, c2])

            def soft(i):
                r, p = softmax_rows(i)
                dp = scr1[r, :]
                inner = jnp.sum(p * dp, axis=1, keepdims=True)
                xs0[r, p_at] = p.astype(bf16)
                xs0[r, ds_at] = (p * (dp - inner)).astype(bf16)

            loop(rows // sub, soft)
            terms = (
                mm(xs0[:, ds_at], half_of(k[:, c2], e)) * 0.125,
                mm_tn(xs0[:, ds_at], q_e),
                mm_tn(xs0[:, p_at], do_e),
            )
            dq, dk, dv = terms if dq is None else (dq + terms[0], dk + terms[1], dv + terms[2])
        q[:, c2] = dq.astype(bf16)
        k[:, c2] = dk.astype(bf16)
        v[:, c2] = dv.astype(bf16)
        small[pl.ds(2, 1), c2] = jnp.sum(q[:, c2].astype(f32), axis=0, keepdims=True)
        small[pl.ds(2, 1), cols(pr + 4)] = jnp.sum(v[:, c2].astype(f32), axis=0, keepdims=True)

    def theirs(m):
        pr = 2 * (1 - core) + m
        attend_back(pr)
        for w, src in enumerate((q, k, v)):
            dqkv_send(w, m, src, pr).start()

    loop(2, theirs)
    sm.step(6)

    def ours(m):
        attend_back(2 * core + m)

    loop(2, ours)
    sm.step(7)
    h1t_out.wait_recv()
    for w, src in enumerate((q, k, v)):
        for m in range(2):
            dqkv_send(w, m, src, m).wait_recv()
        for m in range(2):
            high = pl.ds(m * 512, 512)
            loc_b[8 + 2 * w + m] = (
                mm(h1t[0, high, :], src[:, cols(core, 256)]) + mm(h1t[1, high, :], act_sib[w])
            ).astype(bf16)
    sm.step(8)

    for n in range(4):
        x_send("x1", n, xs1, xr1).wait_recv()

    def finish(i):
        r = pl.ds(pl.multiple_of(i * tile, tile), tile)
        hid[r, :] = (
            y1[r, :] + (xs1[r, :].astype(f32) + xr1[r, :].astype(f32)) + downb[...]
        ).astype(bf16)

    loop(rows // tile, finish)
    lo_out = load(6, hid, lo_h)
    lo_out.start()

    last = wdown.at[pl.ds(0, rows), :]

    def back_one(n):
        c4 = cols(n, 256)
        xs0[:, c4] = (
            mm_nt(q[...], wqkv[0, c4, :]) + mm_nt(k[...], wqkv[1, c4, :]) + mm_nt(v[...], wqkv[2, c4, :])
        ).astype(bf16)
        x_send("x2", n, xs0, last).start()

    loop(width // 256, back_one)
    sm.step(9)
    sm.step(10)
    for n in range(4):
        x_send("x2", n, xs0, last).wait_recv()
    sums[...] = jnp.zeros_like(sums)

    def norm_one_back(i):
        r = pl.ds(pl.multiple_of(i * back, back), back)
        g = xs0[r, :].astype(f32) + wdown[r, :].astype(f32)
        n1, r1 = normed(tok[r, :].astype(f32))
        gn = g * n1
        sums[0] += split_rows(gn)
        sums[1] += split_rows(g)
        e1 = g * again[...]
        m1 = jnp.mean(e1, axis=-1, keepdims=True)
        m2 = jnp.mean(e1 * n1, axis=-1, keepdims=True)
        tok[r, :] = (dy1[r, :] + r1 * (e1 - m1 - n1 * m2)).astype(bf16)

    loop(rows // back, norm_one_back)
    gt_out = load(7, tok, gt_h)
    gt_out.start()
    for i, row in enumerate((0, 1)):
        small[pl.ds(row, 1), :] = jnp.sum(sums[i], axis=0, keepdims=True)

    def small_rc(i, src, to):
        return rc("small", i, src, small_r.at[i], to)

    small_sib = small_rc(0, small, to_sib)
    small_y = small_rc(1, small_r.at[0], to_y)
    small_in = small_rc(2, small_r.at[1], sm.to_z)
    small_mid = small_rc(3, small_r.at[2], sm.to_mid)
    small_out = small_rc(4, small_r.at[3], sm.to_z)
    small_sib.start()
    sm.step(11)
    small_sib.wait_recv()
    small_r[0] += small[...]
    small_y.start()
    sm.step(12)
    small_y.wait_recv()
    small_r[1] += small_r[0]

    @pl.when(sm.outer)
    def _():
        small_in.start()

    sm.step(13)

    @pl.when(sm.mid)
    def _():
        small_in.wait_recv()
        small_r[2] += small_r[1]
        small_mid.start()

    sm.step(14)

    @pl.when(sm.mid)
    def _():
        small_mid.wait_recv()
        small_r[3] += small_r[2]
        small_out.start()

    sm.steps(15, max(sm.na, sm.nb) + STAGES - 1)

    @pl.when(sm.outer)
    def _():
        small_out.wait_recv()

    keep = load(8, small_r.at[jnp.where(sm.outer, 4, 3)], small_h)
    keep.start()

    sm.end()
    w_out.wait_send()
    c_out.wait_send()
    h1t_out.wait_send()
    dyb_out.wait_send()
    for i in range(4):
        o_send(i).wait_send()
        h2t_send(i).wait_send()
        act_send(i).wait_send()
        pre_send(i).wait_send()
        x_send("x1", i, xs1, xr1).wait_send()
        x_send("x2", i, xs0, last).wait_send()
    for m in range(2):
        osib_send(m).wait_send()
        for w, src in enumerate((q, k, v)):
            dqkv_send(w, m, src, m).wait_send()
    small_sib.wait_send()
    small_y.wait_send()

    @pl.when(sm.outer)
    def _():
        small_in.wait_send()

    @pl.when(sm.mid)
    def _():
        small_mid.wait_send()
        small_out.wait_send()

    lo_out.wait()
    gt_out.wait()
    keep.wait()


def layer(clip, vectors, tokens, wqkv, wout, wup, wdown, cot):
    rows, width = tokens.shape
    heads_w = wqkv.shape[2]
    hidden = wup.shape[1]
    big = pl.BlockSpec(memory_space=pl.ANY)
    small = pl.BlockSpec(memory_space=pltpu.VMEM)
    na, nb = 10, 14
    vm = lambda *shape: pltpu.VMEM(shape, bf16)
    vf = lambda *shape: pltpu.VMEM(shape, f32)
    return pl.pallas_call(
        layer_kernel,
        out_shape=(
            jax.ShapeDtypeStruct((rows, width), bf16),
            jax.ShapeDtypeStruct((rows, width), bf16),
            jax.ShapeDtypeStruct((na // 2, 2, 256, width), bf16),
            jax.ShapeDtypeStruct((nb // 2, width, heads_w), bf16),
            jax.ShapeDtypeStruct((16, width), f32),
        ),
        in_specs=[pl.BlockSpec(memory_space=pltpu.SMEM)] + [small] * len(vectors) + [big] * 6,
        out_specs=[big] * 5,
        scratch_shapes=[
            vm(rows, width),
            vm(*wqkv.shape),
            vm(2, *wout.shape),
            vm(*wup.shape),
            vm(*wdown.shape),
            vm(2, rows, width),
            vm(rows, width),
            vm(2, width, rows),
            vm(rows, heads_w),
            vm(rows, heads_w),
            vm(rows, heads_w),
            vm(rows, heads_w),
            vm(rows, heads_w),
            vm(rows, 256),
            vf(rows, width),
            vm(2, width, rows),
            vm(rows, hidden),
            vm(rows, hidden),
            vm(4, rows, 256),
            vm(4, rows, 256),
            vm(rows, width),
            vm(rows, width),
            vm(rows, width),
            vm(rows, width),
            vf(rows, width),
            vm(rows, heads_w),
            vf(rows, rows),
            vf(rows, rows),
            vf(16, width),
            vf(5, 16, width),
            vf(3, 8, width),
            vm(na, 128, width),
            vm(nb, 512, 256),
        ]
        + scratch_of(na, 128, width, nb, 512, 256)
        + [
            pltpu.SemaphoreType.DMA((9,)),
            pltpu.SemaphoreType.DMA((N_LINKS,)),
            pltpu.SemaphoreType.DMA((N_LINKS,)),
        ],
        compiler_params=pltpu.CompilerParams(has_side_effects=True, vmem_limit_bytes=VMEM_BYTES),
        name="layer",
    )(clip, *vectors, tokens, wqkv, wout, wup, wdown, cot)


VMEM_BYTES = 60 << 20


def widen_kernel(a_in, b_in, s_in, down, out, up, qkv, ag, ash, qv, ob, mg, ms, ub, db):
    down[...] = a_in[pl.ds(0, 4)].astype(f32)
    out[...] = a_in[4].astype(f32)
    for j in range(4):
        up[:, pl.ds(j * 512, 512)] = b_in[j].astype(f32)
    qkv[...] = b_in[pl.ds(4, 3)].astype(f32)

    @pl.when(pl.program_id(0) == 0)
    def _():
        for ref, row in ((ag, 0), (ash, 1), (ob, 3), (mg, 4), (ms, 5), (db, 8)):
            ref[...] = s_in[pl.ds(row, 1), :]
        qv[pl.ds(0, 1), :] = s_in[pl.ds(2, 1), pl.ds(0, 512)]
        qv[pl.ds(1, 1), :] = s_in[pl.ds(2, 1), pl.ds(512, 512)]
        ub[:, pl.ds(0, 1024)] = s_in[pl.ds(6, 1), :]
        ub[:, pl.ds(1024, 1024)] = s_in[pl.ds(7, 1), :]


def widen(sum_a, sum_b, small):
    steps = 8
    a = sum_a.reshape(5, 512, 1024)
    whole = lambda *shape: pl.BlockSpec(shape, lambda i: (0,) * len(shape))
    got = pl.pallas_call(
        widen_kernel,
        grid=(steps,),
        in_specs=[
            pl.BlockSpec((5, 512 // steps, 1024), lambda i: (0, i, 0)),
            pl.BlockSpec((7, 1024 // steps, 512), lambda i: (0, i, 0)),
            whole(16, 1024),
        ],
        out_specs=[
            pl.BlockSpec((4, 512 // steps, 1024), lambda i: (0, i, 0)),
            pl.BlockSpec((512 // steps, 1024), lambda i: (i, 0)),
            pl.BlockSpec((1024 // steps, 2048), lambda i: (i, 0)),
            pl.BlockSpec((3, 1024 // steps, 512), lambda i: (0, i, 0)),
            whole(1, 1024), whole(1, 1024), whole(2, 512), whole(1, 1024),
            whole(1, 1024), whole(1, 1024), whole(1, 2048), whole(1, 1024),
        ],
        out_shape=[
            jax.ShapeDtypeStruct((4, 512, 1024), f32),
            jax.ShapeDtypeStruct((512, 1024), f32),
            jax.ShapeDtypeStruct((1024, 2048), f32),
            jax.ShapeDtypeStruct((3, 1024, 512), f32),
        ]
        + [
            jax.ShapeDtypeStruct(s, f32)
            for s in ((1, 1024), (1, 1024), (2, 512), (1, 1024), (1, 1024), (1, 1024), (1, 2048), (1, 1024))
        ],
        compiler_params=pltpu.CompilerParams(vmem_limit_bytes=40 << 20),
        name="widen",
    )(a, sum_b, small)
    down, out, up, qkv, ag, ash, qv, ob, mg, ms, ub, db = got
    flat = lambda v: v.reshape(-1)
    return (
        flat(ag), flat(ash), qkv, qv, out, flat(ob), flat(mg), flat(ms), up, flat(ub),
        down.reshape(2048, 1024), flat(db),
    )


def local(
    tokens, clip_lengths, attn_gain, attn_shift, qkv_weight, qv_bias, out_weight, out_bias,
    mlp_gain, mlp_shift, up_weight, up_bias, down_weight, down_bias, cotangent,
):
    row = lambda v: v.reshape(1, -1)
    vectors = (
        row(attn_gain), row(attn_shift), qv_bias, row(out_bias), row(mlp_gain), row(mlp_shift),
        row(up_bias), row(down_bias),
    )
    layer_output, grad_tokens, sum_a, sum_b, small = layer(
        clip_lengths, vectors, tokens, qkv_weight, out_weight, up_weight, down_weight, cotangent
    )
    groups = lax.axis_size("dp")
    if groups > CELL:
        cells = [[k * CELL + i for k in range(groups // CELL)] for i in range(CELL)]
        wide = (sum_a.astype(f32), sum_b.astype(f32), small)
        sum_a, sum_b, small = lax.psum(wide, "dp", axis_index_groups=cells)
    return (layer_output, grad_tokens, *widen(sum_a, sum_b, small))


def solution(mesh):
    placed = (
        P("dp", None), P("dp", None), P(), P(), P(None, None, "tensor"), P(None, "tensor"),
        P("tensor", None), P(), P(), P(), P(None, "tensor"), P("tensor"), P("tensor", None), P(),
        P("dp", None),
    )
    return jax.shard_map(
        local,
        mesh=mesh,
        in_specs=placed,
        out_specs=(
            P("dp", None), P("dp", None), P(), P(), P(None, None, "tensor"), P(None, "tensor"),
            P("tensor", None), P(), P(), P(), P(None, "tensor"), P("tensor"), P("tensor", None), P(),
        ),
        check_vma=False,
    )
```

time: 469 us -> 263 us (0.56); the launches traced: 463 us -> 262 us
  Pallas kernels: 148 us -> 253 us
  matrix products: 85.1 us -> 0 us
  local copies, waits for them, and re-layouts: 73.1 us -> 8.35 us
  blocking collectives: 62.5 us -> 0 us
  other arithmetic: 59 us -> 0 us
  waiting for transfers between devices: 22.1 us -> 0 us
  starting transfers between devices: 8.89 us -> 0 us
    pallas_call x1 -> x2, Pallas kernels: 148 us -> 253 us  [the longest x1 245 us: layer(): pl.pallas_call(layer_kernel, out_shape=(jax.ShapeDtypeStruct((rows, width...]
    dot_general x24 -> x0, matrix products: 85.1 us -> none  [the longest x6 18.6 us: matmul(): return jnp.dot(left_side, right_side, preferred_element_type=jnp.float32)]
    psum x1 -> x0, blocking collectives: 62.5 us -> none  [local(): lax.psum((attn_gain_grad, attn_shift_grad, qv_grad, out_bias_grad, mlp_ga...]
    select_n x16 -> x0, other arithmetic: 22.5 us -> none  [the longest x4 9.81 us: pair_rows(): first = jnp.where(core == 0, value, other)]
    ppermute x14 -> x0, waiting for transfers between devices: 22.1 us -> none  [the longest x4 21.2 us: over_tensor(): other = lax.ppermute(low, 'tensor', [(0, 1), (1, 0)])]
    unnamed x110 -> x12, local copies, waits for them, and re-layouts: 29.2 us -> 8.35 us
    slice x6 -> x0, local copies, waits for them, and re-layouts: 18.1 us -> none  [the longest x2 11.1 us: pair_cols(): mine = jnp.where(core == 0, halves[:, :, 0], halves[:, :, 1])]
    reduce_sum x9 -> x0, other arithmetic: 16.4 us -> none  [the longest x2 4.99 us: norm_backward(): jnp.sum(grad_rows * normed, axis=0)]
  transfers between devices with their start and end apart: 14 -> 0, of which waited for: 3 -> 0; matrix products, arithmetic and copies ran while one was open for 36% -> 0% of each run, Pallas kernels for 32% -> 0%
where the time goes in v2:
time: 263 us; the launch traced here: 262 us
  Pallas kernels  253 us (96%)
  local copies, waits for them, and re-layouts  8.35 us (3%)
    pallas_call x1, Pallas kernels, layer(): pl.pallas_call(layer_kernel, out_shape=(jax.ShapeDtypeStruct((rows, width...  245 us
    pallas_call x1, Pallas kernels, widen(): pl.pallas_call(widen_kernel, grid=(steps,), in_specs=[pl.BlockSpec((5, 51...  8.84 us
    unnamed x12, local copies, waits for them, and re-layouts  8.35 us

profile of v2, /device:TPU:0, one launch (start us, length us, event | category | flops | bytes accessed | tf_op | source)
XLA Modules:
  0.0 262.4 jit_solution(11201551979317959934)
XLA Ops:
  0.7 244.5 %layer.1 = (bf16[512,1024]{1,0:T(8,128)(2,1)}, bf16[512,1024]{1,0:T(8,128)(2,1)}, bf16[5,2,256,1024]{3,2,1,0:T(8,128)(2,1)}, bf16[7,1024,512]{2,1,0:T(8,128)(2,1)}, f32[16,1024]{1,0:T(8,128)}) custom-call(s32[1,3]{1,0:T(1,128)} %clip.1, f32[1,1024]{1,0:T(1,128)} %bitcast.18, f32[1,1024]{1,0:T(1,128)} %bitcast.19, f32[2,512]{1,0:T(2,128)} %qvb.1, ...), custom_call_target="tpu_custom_call" | custom-call | tf_op jit(solution)/shard_map/layer/pallas_call | solution.py:874
  245.2 0.0 copy-start
  245.2 3.1 %copy-done = bf16[7,1024,512]{2,1,0:T(8,128)(2,1)S(1)} copy-done((bf16[7,1024,512]{2,1,0:T(8,128)(2,1)S(1)}, bf16[7,1024,512]{2,1,0:T(8,128)(2,1)}, u32[]{:S(2)}) %copy-start) | copy-done | bytes 7340056
  248.2 0.0 copy-start.1
  248.2 2.5 copy-done.1
  250.7 0.0 copy-start.2
  250.7 0.8 copy-done.2
  251.6 0.0 copy-start.4
  251.6 0.0 copy-start.3
  251.6 8.8 %widen.1 = (f32[4,512,1024]{2,1,0:T(8,128)}, f32[512,1024]{1,0:T(8,128)}, f32[1024,2048]{1,0:T(8,128)}, f32[3,1024,512]{2,1,0:T(8,128)}, f32[1,1024]{1,0:T(1,128...) custom-call(bf16[5,512,1024]{2,1,0:T(8,128)(2,1)S(1)} %bitcast.16, ...), custom_call_target="tpu_custom_call" | custom-call | tf_op jit(solution)/shard_map/widen/pallas_call | solution.py:955
  260.4 0.0 copy-done.4
  260.4 1.0 copy.31
  261.4 0.0 copy-done.3
  261.4 1.0 copy.32
Async XLA Ops:
  245.2 3.1 %copy-start = (bf16[7,1024,512]{2,1,0:T(8,128)(2,1)S(1)}, bf16[7,1024,512]{2,1,0:T(8,128)(2,1)}, u32[]{:S(2)}) copy-start(bf16[7,1024,512]{2,1,0:T(8,128)(2,1)} %get-tuple-element.34.b_in) | copy-start | bytes 22020100
  248.2 2.5 copy-start.1
  250.7 0.8 copy-start.2
  251.6 8.9 %copy-start.4 = (bf16[512,1024]{1,0:T(8,128)(2,1)S(1)}, bf16[512,1024]{1,0:T(8,128)(2,1)}, u32[]{:S(2)}) copy-start(bf16[512,1024]{1,0:T(8,128)(2,1)} %get-tuple-element.62) | copy-start | bytes 3145732
  251.6 9.8 %copy-start.3 = (bf16[512,1024]{1,0:T(8,128)(2,1)S(1)}, bf16[512,1024]{1,0:T(8,128)(2,1)}, u32[]{:S(2)}) copy-start(bf16[512,1024]{1,0:T(8,128)(2,1)} %get-tuple-element.63) | copy-start | bytes 3145732

commit v3 on v2

--- a/solution.py
+++ b/solution.py
@@ -361,8 +361,8 @@
     clip, again, ashift, qvb, outb, mgain, mshift, upb, downb,
     tok_h, wqkv_h, wout_h, wup_h, wdown_h, cot_h,
     lo_h, gt_h, out_a, out_b, small_h,
-    tok, wqkv, wout, wup, wdown, cpair, hid, h1t, q, k, v, o_own, o_peer, o_sib, y1, h2t,
-    act, pre, act_sib, pre_sib, xs0, xs1, xr0, xr1, dy1, dob, scr0, scr1, small, small_r, sums,
+    tok, wqkv, wout, wup, wdown, cpair, hid, q, k, v, o_own, o_peer, o_sib, y1, h2t,
+    act, pre, act_sib, pre_sib, xs0, xs1, xr0, xr1, dy1, dob, small, small_r, sums,
     loc_a, loc_b, a1, a2, a3, b1, b2, b3,
     as_, ar_, bs_, br_, ls_, lsem, ssem, rsem,
 ):
@@ -383,12 +383,12 @@
     def cols(i, n=128):
         return pl.ds(pl.multiple_of(i * n, n), n)
 
-    def loop(n, body):
+    def loop(n, body, unroll=False):
         def wrapped(i, _):
             body(i)
             return 0
 
-        lax.fori_loop(0, n, wrapped, 0)
+        lax.fori_loop(0, n, wrapped, 0, unroll=unroll)
 
     def load(i, src, dst):
         return pltpu.make_async_copy(src, dst, lsem.at[i])
@@ -432,7 +432,7 @@
         n1, _ = normed(tok[r, :].astype(f32))
         hid[r, :] = (n1 * again[...] + ashift[...]).astype(bf16)
 
-    loop(rows // tile, norm_one)
+    loop(rows // tile, norm_one, True)
     loads[1].wait()
     heads_w = q.shape[1]
     lane = lax.broadcasted_iota(jnp.int32, (1, 128), 1)
@@ -450,14 +450,13 @@
         return one(end0) + one(end1) + one(end2)
 
     key_seg = seg_of(lax.broadcasted_iota(jnp.int32, (1, rows), 1))
-    sub = 32
-
-    def softmax_rows(i):
-        r = pl.ds(pl.multiple_of(i * sub, sub), sub)
-        row_seg = seg_of(lax.broadcasted_iota(jnp.int32, (sub, 1), 0) + i * sub)
-        s = jnp.where(row_seg == key_seg, scr0[r, :], -1e30)
+    def same_clip(at, count):
+        return seg_of(lax.broadcasted_iota(jnp.int32, (count, 1), 0) + at) == key_seg
+
+    def softmax(products, same):
+        s = jnp.where(same, products, -1e30)
         w = jnp.exp(s - jnp.max(s, axis=1, keepdims=True))
-        return r, w * (1.0 / jnp.sum(w, axis=1, keepdims=True))
+        return w * (1.0 / jnp.sum(w, axis=1, keepdims=True))
 
     def make_qkv(g):
         c4 = cols(g, 256)
@@ -475,18 +474,17 @@
 
     def attend(pr):
         c2 = cols(pr)
-        total = None
-        for e in range(2):
-            scr0[...] = mm_nt(half_of(q[:, c2], e), k[:, c2])
-
-            def soft(i):
-                r, p = softmax_rows(i)
-                xs0[r, pl.ds(0, rows)] = p.astype(bf16)
-
-            loop(rows // sub, soft)
-            term = mm(xs0[:, pl.ds(0, rows)], half_of(v[:, c2], e))
-            total = term if total is None else total + term
-        o_own[:, c2] = total.astype(bf16)
+        keys = k[:, c2]
+        values = [half_of(v[:, c2], e) for e in range(2)]
+        for at in range(0, rows, 256):
+            r = pl.ds(at, 256)
+            same = same_clip(at, 256)
+            total = None
+            for e in range(2):
+                p = softmax(mm_nt(half_of(q[r, c2], e), keys), same)
+                term = mm(p.astype(bf16), values[e])
+                total = term if total is None else total + term
+            o_own[r, c2] = total.astype(bf16)
         o_send(pr).start()
 
         @pl.when(pr // 2 == 1 - core)
@@ -510,7 +508,7 @@
         r = pl.ds(pl.multiple_of(i * nrow, nrow), nrow)
         y1[r, :] = mm(o_own[r, :], wout[t])
 
-    loop(rows // nrow, own_part)
+    loop(rows // nrow, own_part, True)
     w_y.wait_recv()
     w_s1.start()
     w_s0.wait_recv()
@@ -521,13 +519,19 @@
     for pr in range(4):
         o_send(pr).wait_recv()
 
+    def peer_part(i):
+        r = pl.ds(pl.multiple_of(i * nrow, nrow), nrow)
+        dy1[r, :] = mm(o_peer[r, :], wout[1 - t])
+
+    loop(rows // nrow, peer_part, True)
+
     def h2t_send(i):
         return rc("h2t", i, h2t.at[0, :, cols(i, nrow)], h2t.at[1, :, cols(i, nrow)], to_sib)
 
     def norm_two(i):
         r = pl.ds(pl.multiple_of(i * nrow, nrow), nrow)
         x = tok[r, :].astype(f32)
-        y = x + (y1[r, :] + mm(o_peer[r, :], wout[1 - t])) + outb[...]
+        y = x + (y1[r, :] + dy1[r, :]) + outb[...]
         y1[r, :] = y
         n2, _ = normed(y)
         h2 = (n2 * mgain[...] + mshift[...]).astype(bf16)
@@ -536,7 +540,7 @@
         h2t_send(i).start()
 
     hid_two = xs1
-    loop(rows // nrow, norm_two)
+    loop(rows // nrow, norm_two, True)
 
     loads[3].wait()
     loads[4].wait()
@@ -553,19 +557,11 @@
 
     def hidden(piece):
         c4 = cols(piece, 256)
-        half = pl.ds(0, 256)
-        scr0[:, half] = mm(hid_two[...], wup[:, c4]) + upb[:, c4]
-        scr1[:, half] = mm_nt(cpair[0], wdown[c4, :])
-
-        def slope(i, total):
-            r = pl.ds(pl.multiple_of(i * tile, tile), tile)
-            a, d = gelu_parts(scr0[r, half])
-            du = (scr1[r, half] * d).astype(bf16)
-            act[r, c4] = a.astype(bf16)
-            pre[r, c4] = du
-            return total + split_rows(du.astype(f32))
-
-        total = lax.fori_loop(0, rows // tile, slope, jnp.zeros((8, 256), f32))
+        a, d = gelu_parts(mm(hid_two[...], wup[:, c4]) + upb[:, c4])
+        du = (mm_nt(cpair[0], wdown[c4, :]) * d).astype(bf16)
+        act[:, c4] = a.astype(bf16)
+        pre[:, c4] = du
+        total = split_rows(du.astype(f32))
         row = 6 + piece // 4
         small[pl.ds(row, 1), cols(lax.rem(piece, 4), 256)] = jnp.sum(total, axis=0, keepdims=True)
 
@@ -617,19 +613,22 @@
 
     loop(width // 256, forward_two)
 
+    for i in range(4):
+        h2t_send(i).wait_send()
+    h1t = h2t
+
     def turn_first(i):
         r = pl.ds(pl.multiple_of(i * nrow, nrow), nrow)
         h1t[0, :, cols(i, nrow)] = hid[r, :].T
 
-    loop(rows // nrow, turn_first)
+    loop(rows // nrow, turn_first, True)
     h1t_out = rc("h1t", 0, h1t.at[0], h1t.at[1], to_sib)
-    h1t_out.start()
 
     def cot_sum(i, total):
         r = pl.ds(pl.multiple_of(i * tile, tile), tile)
         return total + split_rows(cpair[0, r, :].astype(f32))
 
-    total = lax.fori_loop(0, rows // tile, cot_sum, jnp.zeros((8, width), f32))
+    total = lax.fori_loop(0, rows // tile, cot_sum, jnp.zeros((8, width), f32), unroll=True)
     small[pl.ds(8, 1), :] = jnp.sum(total, axis=0, keepdims=True)
     sm.step(3)
     sm.step(4)
@@ -637,7 +636,7 @@
     for n in range(4):
         x_send("x0", n, xs0, xr0).wait_recv()
     sums[...] = jnp.zeros_like(sums)
-    back = 32
+    back = 128
     dyb = xr0
 
     def norm_two_back(i):
@@ -671,6 +670,7 @@
     osib_send(0).wait_recv()
     osib_send(1).wait_recv()
     dyb_out.wait_recv()
+    h1t_out.start()
     for n in range(width // 512):
         wide = pl.ds(n * 512, 512)
         low = (
@@ -684,25 +684,17 @@
 
     def attend_back(pr):
         c2 = cols(pr)
-        p_at, ds_at = pl.ds(0, rows), pl.ds(rows, rows)
+        same = same_clip(0, rows)
         dq = dk = dv = None
         for e in range(2):
             q_e, do_e = half_of(q[:, c2], e), half_of(dob[:, c2], e)
-            scr0[...] = mm_nt(q_e, k[:, c2])
-            scr1[...] = mm_nt(do_e, v[:, c2])
-
-            def soft(i):
-                r, p = softmax_rows(i)
-                dp = scr1[r, :]
-                inner = jnp.sum(p * dp, axis=1, keepdims=True)
-                xs0[r, p_at] = p.astype(bf16)
-                xs0[r, ds_at] = (p * (dp - inner)).astype(bf16)
-
-            loop(rows // sub, soft)
+            p = softmax(mm_nt(q_e, k[:, c2]), same)
+            dp = mm_nt(do_e, v[:, c2])
+            ds = (p * (dp - jnp.sum(p * dp, axis=1, keepdims=True))).astype(bf16)
             terms = (
-                mm(xs0[:, ds_at], half_of(k[:, c2], e)) * 0.125,
-                mm_tn(xs0[:, ds_at], q_e),
-                mm_tn(xs0[:, p_at], do_e),
+                mm(ds, half_of(k[:, c2], e)) * 0.125,
+                mm_tn(ds, q_e),
+                mm_tn(p.astype(bf16), do_e),
             )
             dq, dk, dv = terms if dq is None else (dq + terms[0], dk + terms[1], dv + terms[2])
         q[:, c2] = dq.astype(bf16)
@@ -745,7 +737,7 @@
             y1[r, :] + (xs1[r, :].astype(f32) + xr1[r, :].astype(f32)) + downb[...]
         ).astype(bf16)
 
-    loop(rows // tile, finish)
+    loop(rows // tile, finish, True)
     lo_out = load(6, hid, lo_h)
     lo_out.start()
 
@@ -836,7 +828,6 @@
     dyb_out.wait_send()
     for i in range(4):
         o_send(i).wait_send()
-        h2t_send(i).wait_send()
         act_send(i).wait_send()
         pre_send(i).wait_send()
         x_send("x1", i, xs1, xr1).wait_send()
@@ -890,7 +881,6 @@
             vm(*wdown.shape),
             vm(2, rows, width),
             vm(rows, width),
-            vm(2, width, rows),
             vm(rows, heads_w),
             vm(rows, heads_w),
             vm(rows, heads_w),
@@ -909,8 +899,6 @@
             vm(rows, width),
             vf(rows, width),
             vm(rows, heads_w),
-            vf(rows, rows),
-            vf(rows, rows),
             vf(16, width),
             vf(5, 16, width),
             vf(3, 8, width),
@@ -978,7 +966,7 @@
             jax.ShapeDtypeStruct(s, f32)
             for s in ((1, 1024), (1, 1024), (2, 512), (1, 1024), (1, 1024), (1, 1024), (1, 2048), (1, 1024))
         ],
-        compiler_params=pltpu.CompilerParams(vmem_limit_bytes=40 << 20),
+        compiler_params=pltpu.CompilerParams(vmem_limit_bytes=56 << 20),
         name="widen",
     )(a, sum_b, small)
     down, out, up, qkv, ag, ash, qv, ob, mg, ms, ub, db = got

time: 263 us -> 198 us (0.75)
  Pallas kernels: 253 us -> 195 us
  local copies, waits for them, and re-layouts: 8.35 us -> 1.95 us
    pallas_call x1, Pallas kernels: 245 us -> 181 us  [layer(): pl.pallas_call(layer_kernel, out_shape=(jax.ShapeDtypeStruct((rows, width...]
    unnamed x12 -> x6, local copies, waits for them, and re-layouts: 8.35 us -> 1.95 us
    pallas_call x1, Pallas kernels: 8.84 us -> 14.3 us  [widen(): pl.pallas_call(widen_kernel, grid=(steps,), in_specs=[pl.BlockSpec((5, 51...]
where the time goes in v3:
time: 198 us
  Pallas kernels  195 us (98%)
    pallas_call x1, Pallas kernels, layer(): pl.pallas_call(layer_kernel, out_shape=(jax.ShapeDtypeStruct((rows, width...  181 us
    pallas_call x1, Pallas kernels, widen(): pl.pallas_call(widen_kernel, grid=(steps,), in_specs=[pl.BlockSpec((5, 51...  14.3 us

profile of v3, /device:TPU:0, one launch (start us, length us, event | category | flops | bytes accessed | tf_op | source)
XLA Modules:
  0.0 197.7 jit_solution(6928523145355760678)
XLA Ops:
  0.7 180.8 %layer.1 = (bf16[512,1024]{1,0:T(8,128)(2,1)}, bf16[512,1024]{1,0:T(8,128)(2,1)}, bf16[5,2,256,1024]{3,2,1,0:T(8,128)(2,1)}, bf16[7,1024,512]{2,1,0:T(8,128)(2,1)}, f32[16,1024]{1,0:T(8,128)}) custom-call(s32[1,3]{1,0:T(1,128)} %clip.1, f32[1,1024]{1,0:T(1,128)} %bitcast.18, f32[1,1024]{1,0:T(1,128)} %bitcast.19, f32[2,512]{1,0:T(2,128)} %qvb.1, ...), custom_call_target="tpu_custom_call" | custom-call | tf_op jit(solution)/shard_map/layer/pallas_call | solution.py:865
  181.4 0.0 copy-start.1
  181.5 0.0 copy-start
  181.5 14.3 %widen.1 = (f32[4,512,1024]{2,1,0:T(8,128)}, f32[512,1024]{1,0:T(8,128)}, f32[1024,2048]{1,0:T(8,128)}, f32[3,1024,512]{2,1,0:T(8,128)}, f32[1,1024]{1,0:T(1,128...) custom-call(bf16[5,512,1024]{2,1,0:T(8,128)(2,1)} %bitcast.16, ...), custom_call_target="tpu_custom_call" | custom-call | tf_op jit(solution)/shard_map/widen/pallas_call | solution.py:943
  195.7 0.0 copy-done.1
  195.7 1.0 copy.31
  196.7 0.0 copy-done
  196.7 1.0 copy.32
Async XLA Ops:
  181.4 14.3 %copy-start.1 = (bf16[512,1024]{1,0:T(8,128)(2,1)S(1)}, bf16[512,1024]{1,0:T(8,128)(2,1)}, u32[]{:S(2)}) copy-start(bf16[512,1024]{1,0:T(8,128)(2,1)} %get-tuple-element.62) | copy-start | bytes 3145732
  181.5 15.3 %copy-start = (bf16[512,1024]{1,0:T(8,128)(2,1)S(1)}, bf16[512,1024]{1,0:T(8,128)(2,1)}, u32[]{:S(2)}) copy-start(bf16[512,1024]{1,0:T(8,128)(2,1)} %get-tuple-element.63) | copy-start | bytes 3145732

commit v4 on v3

--- a/solution.py
+++ b/solution.py
@@ -9,6 +9,23 @@
 bf16, f32 = jnp.bfloat16, jnp.float32
 CELL = 16
 STAGES = 6
+SIDE = 256
+N_DOWN = N_UP = 16
+CHUNKS = 24
+
+
+def pick(low, first, second):
+    if isinstance(low, bool):
+        return first if low else second
+    return jnp.where(low, first, second)
+
+
+def place_a(i):
+    return pick(i < N_DOWN, i, i + N_UP)
+
+
+def place_b(i):
+    return pick(i < N_UP, i + N_DOWN, i + CHUNKS)
 
 
 def place():
@@ -22,13 +39,11 @@
 
 
 class Summer:
-    def __init__(self, loc_a, loc_b, bufs, out_a, out_b, sems):
+    def __init__(self, loc_a, loc_b, bufs, out, sems):
         self.loc_a, self.loc_b = loc_a, loc_b
         (self.a1, self.a2, self.a3, self.b1, self.b2, self.b3) = bufs
-        self.out_a, self.out_b = out_a, out_b
+        self.out = out
         self.as_, self.ar_, self.bs_, self.br_, self.ls_ = sems
-        self.na = loc_a.shape[0]
-        self.nb = loc_b.shape[0]
         self.ha = loc_a.shape[1] // 2
         self.hb = loc_b.shape[1] // 2
         base, z, y, core = place()
@@ -55,16 +70,13 @@
         return self.loc_b.at[i, pl.ds(pl.multiple_of(h * self.hb, self.hb), self.hb), :]
 
     def oa(self, i, h, core):
-        at = lax.rem(i, 2) * 2 * self.ha + h * self.ha
-        return self.out_a.at[i // 2, core, pl.ds(pl.multiple_of(at, self.ha), self.ha), :]
+        return self.out.at[
+            place_a(i), core, pl.ds(pl.multiple_of(h * self.ha, self.ha), self.ha), :
+        ]
 
     def ob(self, i, h, core):
-        w = self.loc_b.shape[2]
-        at = lax.rem(i, 2) * 2 * self.hb + h * self.hb
-        return self.out_b.at[
-            i // 2,
-            pl.ds(pl.multiple_of(at, self.hb), self.hb),
-            pl.ds(pl.multiple_of(core * w, w), w),
+        return self.out.at[
+            place_b(i), core, pl.ds(pl.multiple_of(h * self.hb, self.hb), self.hb), :
         ]
 
     def ca(self, i, kind, recv, src, dst, to):
@@ -247,16 +259,21 @@
         self.b_done(i, 6, 6, fin, mine, self.to_sib).wait_recv()
 
     def step(self, t):
-        for stage in range(STAGES):
+        for stage in (*range(STAGES), STAGES + 1):
             i = t - stage
 
-            @pl.when(jnp.logical_and(i >= 0, i < self.na))
-            def _():
-                self.step_a(i, stage)
-
-            @pl.when(jnp.logical_and(i >= 0, i < self.nb))
-            def _():
-                self.step_b(i, stage)
+            def run():
+                if stage < STAGES:
+                    self.step_a(i, stage)
+                    self.step_b(i, stage)
+                else:
+                    self.end_a(i)
+                    self.end_b(i)
+
+            if not isinstance(t, int):
+                pl.when(jnp.logical_and(i >= 0, i < CHUNKS))(run)
+            elif 0 <= i < CHUNKS:
+                run()
 
     def steps(self, lo, hi):
         def body(t, _):
@@ -266,31 +283,30 @@
         lax.fori_loop(lo, hi, body, 0)
 
     def end(self):
-        def body_a(i, _):
+        def body(i, _):
             self.end_a(i)
-            return 0
-
-        def body_b(i, _):
             self.end_b(i)
             return 0
 
-        lax.fori_loop(0, self.na, body_a, 0)
-        lax.fori_loop(0, self.nb, body_b, 0)
-
-
-def scratch_of(na, ra, wa, nb, rb, wb):
+        lax.fori_loop(CHUNKS - 2, CHUNKS, body, 0)
+
+
+def scratch_of(n, side):
+    whole, half = pltpu.VMEM((n, side, side), bf16), pltpu.VMEM((n, side // 2, side), bf16)
     return [
-        pltpu.VMEM((na, ra // 2, wa), bf16),
-        pltpu.VMEM((na, ra // 2, wa), bf16),
-        pltpu.VMEM((na, ra // 2, wa), bf16),
-        pltpu.VMEM((nb, rb, wb), bf16),
-        pltpu.VMEM((nb, rb // 2, wb), bf16),
-        pltpu.VMEM((nb, rb // 2, wb), bf16),
-        pltpu.SemaphoreType.DMA((na, 6)),
-        pltpu.SemaphoreType.DMA((na, 7)),
-        pltpu.SemaphoreType.DMA((nb, 7)),
-        pltpu.SemaphoreType.DMA((nb, 7)),
-        pltpu.SemaphoreType.DMA((2, max(na, nb))),
+        whole,
+        whole,
+        half,
+        half,
+        half,
+        whole,
+        half,
+        half,
+        pltpu.SemaphoreType.DMA((n, 6)),
+        pltpu.SemaphoreType.DMA((n, 7)),
+        pltpu.SemaphoreType.DMA((n, 7)),
+        pltpu.SemaphoreType.DMA((n, 7)),
+        pltpu.SemaphoreType.DMA((2, n)),
     ]
 
 
@@ -360,7 +376,7 @@
 def layer_kernel(
     clip, again, ashift, qvb, outb, mgain, mshift, upb, downb,
     tok_h, wqkv_h, wout_h, wup_h, wdown_h, cot_h,
-    lo_h, gt_h, out_a, out_b, small_h,
+    lo_h, gt_h, out, small_h,
     tok, wqkv, wout, wup, wdown, cpair, hid, q, k, v, o_own, o_peer, o_sib, y1, h2t,
     act, pre, act_sib, pre_sib, xs0, xs1, xr0, xr1, dy1, dob, small, small_r, sums,
     loc_a, loc_b, a1, a2, a3, b1, b2, b3,
@@ -368,7 +384,7 @@
 ):
     rows = tok.shape[0]
     width = tok.shape[1]
-    sm = Summer(loc_a, loc_b, (a1, a2, a3, b1, b2, b3), out_a, out_b, (as_, ar_, bs_, br_, ls_))
+    sm = Summer(loc_a, loc_b, (a1, a2, a3, b1, b2, b3), out, (as_, ar_, bs_, br_, ls_))
     base, z, y, core = place()
     t = lax.axis_index("tensor")
     to_x = (lax.axis_index("dp"), 1 - t)
@@ -417,12 +433,20 @@
     other = 2 * (1 - y) + core
     w_s1 = rc("w", 3, w_at(other), w_at(other), to_sib)
     c_out = rc("c", 0, cot_h, cpair.at[1], to_sib)
-    loads[0].start()
-    loads[1].start()
-    w_out.start()
-    for item in loads[2:]:
+    for item in loads:
         item.start()
-    c_out.start()
+
+    barrier = pltpu.get_barrier_semaphore()
+
+    def greet(to):
+        pl.semaphore_signal(barrier, inc=1, device_id=to, device_id_type=MESH)
+
+    for to in (to_sib, to_x, to_y, sm.to_z):
+        greet(to)
+
+    @pl.when(sm.mid)
+    def _():
+        greet(sm.to_mid)
 
     loads[0].wait()
     tile = 64
@@ -433,6 +457,17 @@
         hid[r, :] = (n1 * again[...] + ashift[...]).astype(bf16)
 
     loop(rows // tile, norm_one, True)
+
+    @pl.when(sm.mid)
+    def _():
+        pl.semaphore_wait(barrier, 5)
+
+    @pl.when(sm.outer)
+    def _():
+        pl.semaphore_wait(barrier, 4)
+
+    w_out.start()
+    c_out.start()
     loads[1].wait()
     heads_w = q.shape[1]
     lane = lax.broadcasted_iota(jnp.int32, (1, 128), 1)
@@ -565,37 +600,37 @@
         row = 6 + piece // 4
         small[pl.ds(row, 1), cols(lax.rem(piece, 4), 256)] = jnp.sum(total, axis=0, keepdims=True)
 
-    def chunk(j):
+    def chunk(j, middle=None):
         hidden(2 * j + 1 - core)
         act_send(j).start()
         pre_send(j).start()
         hidden(2 * j + core)
+        if middle is not None:
+            sm.step(middle)
         mine = cols(2 * j + core, 256)
         act_send(j).wait_recv()
-        for n in range(width // 512):
+        for n in range(2):
             wide = pl.ds(n * 512, 512)
             block = mm_tn(act[:, mine], cpair[0, :, wide]) + mm_tn(act_sib[j], cpair[1, :, wide])
             low = block.astype(bf16)
-            loc_a[2 * j, :, wide] = low[:128]
-            loc_a[2 * j + 1, :, wide] = low[128:]
+            loc_a[4 * j + 2 * n] = low[:, :256]
+            loc_a[4 * j + 2 * n + 1] = low[:, 256:]
         pre_send(j).wait_recv()
         for m in range(2):
             high = pl.ds(m * 512, 512)
-            loc_b[2 * j + m] = (
-                mm(h2t[0, high, :], pre[:, mine]) + mm(h2t[1, high, :], pre_sib[j])
-            ).astype(bf16)
-
-    def first_wait():
-        for i in range(4):
-            h2t_send(i).wait_recv()
-
-    first_wait()
+            low = (mm(h2t[0, high, :], pre[:, mine]) + mm(h2t[1, high, :], pre_sib[j])).astype(bf16)
+            loc_b[4 * j + 2 * m] = low[:256]
+            loc_b[4 * j + 2 * m + 1] = low[256:]
+
+    for i in range(4):
+        h2t_send(i).wait_recv()
     chunk(0)
     sm.step(0)
-    chunk(1)
-    chunk(2)
-    sm.step(1)
-    chunk(3)
+    chunk(1, 1)
+    sm.step(2)
+    chunk(2, 3)
+    chunk(3, 4)
+    sm.step(5)
 
     def x_send(name, n, src, dst):
         return rc(name, n, src.at[:, cols(n, 256)], dst.at[:, cols(n, 256)], to_x)
@@ -605,13 +640,14 @@
         x_send("x0", n, xs0, xr0).start()
 
     loop(width // 256, back_two)
-    sm.step(2)
+    sm.step(6)
 
     def forward_two(n):
         xs1[:, cols(n, 256)] = mm(act[...], wdown[:, cols(n, 256)]).astype(bf16)
         x_send("x1", n, xs1, xr1).start()
 
     loop(width // 256, forward_two)
+    sm.step(7)
 
     for i in range(4):
         h2t_send(i).wait_send()
@@ -630,8 +666,7 @@
 
     total = lax.fori_loop(0, rows // tile, cot_sum, jnp.zeros((8, width), f32), unroll=True)
     small[pl.ds(8, 1), :] = jnp.sum(total, axis=0, keepdims=True)
-    sm.step(3)
-    sm.step(4)
+    sm.steps(8, 13)
 
     for n in range(4):
         x_send("x0", n, xs0, xr0).wait_recv()
@@ -666,7 +701,7 @@
         dob[:, cols(n, 256)] = mm_nt(dyb[...], wout[t, cols(n, 256), :]).astype(bf16)
 
     loop(heads_w // 256, back_heads)
-    sm.step(5)
+    sm.step(13)
     osib_send(0).wait_recv()
     osib_send(1).wait_recv()
     dyb_out.wait_recv()
@@ -676,8 +711,10 @@
         low = (
             mm_tn(o_own[:, cols(core, 256)], dyb[:, wide]) + mm_tn(o_sib[...], wout[1 - t, :, wide])
         ).astype(bf16)
-        loc_a[8, :, wide] = low[:128]
-        loc_a[9, :, wide] = low[128:]
+        loc_a[16 + 2 * n] = low[:, :256]
+        loc_a[17 + 2 * n] = low[:, 256:]
+
+    sm.step(14)
 
     def dqkv_send(w, m, src, pr):
         return rc("dqkv", 2 * w + m, src.at[:, cols(pr)], act_sib.at[w, :, cols(m)], to_sib)
@@ -710,38 +747,27 @@
             dqkv_send(w, m, src, pr).start()
 
     loop(2, theirs)
-    sm.step(6)
+    sm.step(15)
 
     def ours(m):
         attend_back(2 * core + m)
 
     loop(2, ours)
-    sm.step(7)
     h1t_out.wait_recv()
     for w, src in enumerate((q, k, v)):
         for m in range(2):
             dqkv_send(w, m, src, m).wait_recv()
-        for m in range(2):
-            high = pl.ds(m * 512, 512)
-            loc_b[8 + 2 * w + m] = (
-                mm(h1t[0, high, :], src[:, cols(core, 256)]) + mm(h1t[1, high, :], act_sib[w])
-            ).astype(bf16)
-    sm.step(8)
-
-    for n in range(4):
-        x_send("x1", n, xs1, xr1).wait_recv()
-
-    def finish(i):
-        r = pl.ds(pl.multiple_of(i * tile, tile), tile)
-        hid[r, :] = (
-            y1[r, :] + (xs1[r, :].astype(f32) + xr1[r, :].astype(f32)) + downb[...]
-        ).astype(bf16)
-
-    loop(rows // tile, finish, True)
-    lo_out = load(6, hid, lo_h)
-    lo_out.start()
-
-    last = wdown.at[pl.ds(0, rows), :]
+        for m in range(4):
+            high = pl.ds(m * 256, 256)
+            low = mm(h1t[0, high, :], src[:, cols(core, 256)]) + mm(h1t[1, high, :], act_sib[w])
+            at = 3 * m + w
+            if at < 4:
+                loc_a[20 + at] = low.astype(bf16)
+            else:
+                loc_b[12 + at] = low.astype(bf16)
+    sm.step(16)
+
+    last = wup.at[pl.ds(0, rows), pl.ds(0, width)]
 
     def back_one(n):
         c4 = cols(n, 256)
@@ -751,15 +777,29 @@
         x_send("x2", n, xs0, last).start()
 
     loop(width // 256, back_one)
-    sm.step(9)
-    sm.step(10)
+    sm.steps(17, 20)
+
+    for n in range(4):
+        x_send("x1", n, xs1, xr1).wait_recv()
+
+    def finish(i):
+        r = pl.ds(pl.multiple_of(i * tile, tile), tile)
+        hid[r, :] = (
+            y1[r, :] + (xs1[r, :].astype(f32) + xr1[r, :].astype(f32)) + downb[...]
+        ).astype(bf16)
+
+    loop(rows // tile, finish, True)
+    lo_out = load(6, hid, lo_h)
+    lo_out.start()
+
+    sm.steps(20, 23)
     for n in range(4):
         x_send("x2", n, xs0, last).wait_recv()
     sums[...] = jnp.zeros_like(sums)
 
     def norm_one_back(i):
         r = pl.ds(pl.multiple_of(i * back, back), back)
-        g = xs0[r, :].astype(f32) + wdown[r, :].astype(f32)
+        g = xs0[r, :].astype(f32) + last[r, :].astype(f32)
         n1, r1 = normed(tok[r, :].astype(f32))
         gn = g * n1
         sums[0] += split_rows(gn)
@@ -784,11 +824,11 @@
     small_mid = small_rc(3, small_r.at[2], sm.to_mid)
     small_out = small_rc(4, small_r.at[3], sm.to_z)
     small_sib.start()
-    sm.step(11)
+    sm.step(23)
     small_sib.wait_recv()
     small_r[0] += small[...]
     small_y.start()
-    sm.step(12)
+    sm.step(24)
     small_y.wait_recv()
     small_r[1] += small_r[0]
 
@@ -796,7 +836,7 @@
     def _():
         small_in.start()
 
-    sm.step(13)
+    sm.step(25)
 
     @pl.when(sm.mid)
     def _():
@@ -804,7 +844,7 @@
         small_r[2] += small_r[1]
         small_mid.start()
 
-    sm.step(14)
+    sm.step(26)
 
     @pl.when(sm.mid)
     def _():
@@ -812,7 +852,7 @@
         small_r[3] += small_r[2]
         small_out.start()
 
-    sm.steps(15, max(sm.na, sm.nb) + STAGES - 1)
+    sm.steps(27, CHUNKS + STAGES - 1)
 
     @pl.when(sm.outer)
     def _():
@@ -859,7 +899,6 @@
     hidden = wup.shape[1]
     big = pl.BlockSpec(memory_space=pl.ANY)
     small = pl.BlockSpec(memory_space=pltpu.VMEM)
-    na, nb = 10, 14
     vm = lambda *shape: pltpu.VMEM(shape, bf16)
     vf = lambda *shape: pltpu.VMEM(shape, f32)
     return pl.pallas_call(
@@ -867,12 +906,11 @@
         out_shape=(
             jax.ShapeDtypeStruct((rows, width), bf16),
             jax.ShapeDtypeStruct((rows, width), bf16),
-            jax.ShapeDtypeStruct((na // 2, 2, 256, width), bf16),
-            jax.ShapeDtypeStruct((nb // 2, width, heads_w), bf16),
+            jax.ShapeDtypeStruct((2 * CHUNKS, 2, SIDE, SIDE), bf16),
             jax.ShapeDtypeStruct((16, width), f32),
         ),
         in_specs=[pl.BlockSpec(memory_space=pltpu.SMEM)] + [small] * len(vectors) + [big] * 6,
-        out_specs=[big] * 5,
+        out_specs=[big] * 4,
         scratch_shapes=[
             vm(rows, width),
             vm(*wqkv.shape),
@@ -902,16 +940,16 @@
             vf(16, width),
             vf(5, 16, width),
             vf(3, 8, width),
-            vm(na, 128, width),
-            vm(nb, 512, 256),
         ]
-        + scratch_of(na, 128, width, nb, 512, 256)
+        + scratch_of(CHUNKS, SIDE)
         + [
             pltpu.SemaphoreType.DMA((9,)),
             pltpu.SemaphoreType.DMA((N_LINKS,)),
             pltpu.SemaphoreType.DMA((N_LINKS,)),
         ],
-        compiler_params=pltpu.CompilerParams(has_side_effects=True, vmem_limit_bytes=VMEM_BYTES),
+        compiler_params=pltpu.CompilerParams(
+            has_side_effects=True, collective_id=0, vmem_limit_bytes=VMEM_BYTES
+        ),
         name="layer",
     )(clip, *vectors, tokens, wqkv, wout, wup, wdown, cot)
 
@@ -919,14 +957,25 @@
 VMEM_BYTES = 60 << 20
 
 
-def widen_kernel(a_in, b_in, s_in, down, out, up, qkv, ag, ash, qv, ob, mg, ms, ub, db):
-    down[...] = a_in[pl.ds(0, 4)].astype(f32)
-    out[...] = a_in[4].astype(f32)
-    for j in range(4):
-        up[:, pl.ds(j * 512, 512)] = b_in[j].astype(f32)
-    qkv[...] = b_in[pl.ds(4, 3)].astype(f32)
-
-    @pl.when(pl.program_id(0) == 0)
+STEPS = 8
+
+
+def widen_kernel(
+    down_in, up_in, out_in, qkv_in, s_in, lo_in, gt_in,
+    lo, gt, down, out, up, qkv, ag, ash, qv, ob, mg, ms, ub, db,
+):
+    lo[...] = lo_in[...]
+    gt[...] = gt_in[...]
+    for n in range(4):
+        c = pl.ds(n * SIDE, SIDE)
+        down[:, c] = down_in[n, 0].astype(f32)
+        out[:, c] = out_in[n, 0].astype(f32)
+        up[c, :] = up_in[n, 0].astype(f32)
+    for w in range(3):
+        for core in range(2):
+            qkv[w, :, pl.ds(core * SIDE, SIDE)] = qkv_in[w, core].astype(f32)
+
+    @pl.when(pl.program_id(0) == STEPS - 1)
     def _():
         for ref, row in ((ag, 0), (ash, 1), (ob, 3), (mg, 4), (ms, 5), (db, 8)):
             ref[...] = s_in[pl.ds(row, 1), :]
@@ -936,44 +985,48 @@
         ub[:, pl.ds(1024, 1024)] = s_in[pl.ds(7, 1), :]
 
 
-def widen(sum_a, sum_b, small):
-    steps = 8
-    a = sum_a.reshape(5, 512, 1024)
+def widen(sums, small, lo, gt):
     whole = lambda *shape: pl.BlockSpec(shape, lambda i: (0,) * len(shape))
+    rows_in = pl.BlockSpec((lo.shape[0] // STEPS, lo.shape[1]), lambda i: (i, 0))
+    vectors = ((1, 1024), (1, 1024), (2, 512), (1, 1024), (1, 1024), (1, 1024), (1, 2048), (1, 1024))
     got = pl.pallas_call(
         widen_kernel,
-        grid=(steps,),
+        grid=(STEPS,),
         in_specs=[
-            pl.BlockSpec((5, 512 // steps, 1024), lambda i: (0, i, 0)),
-            pl.BlockSpec((7, 1024 // steps, 512), lambda i: (0, i, 0)),
+            pl.BlockSpec((4, 1, SIDE, SIDE), lambda i: (i // 2, i % 2, 0, 0)),
+            pl.BlockSpec((4, 1, SIDE, SIDE), lambda i: (4 + i // 2, i % 2, 0, 0)),
+            pl.BlockSpec((4, 1, SIDE // 4, SIDE), lambda i: (8, i // 4, i % 4, 0)),
+            pl.BlockSpec((3, 2, SIDE // 2, SIDE), lambda i: (12 + i // 2, 0, i % 2, 0)),
             whole(16, 1024),
+            rows_in,
+            rows_in,
         ],
         out_specs=[
-            pl.BlockSpec((4, 512 // steps, 1024), lambda i: (0, i, 0)),
-            pl.BlockSpec((512 // steps, 1024), lambda i: (i, 0)),
-            pl.BlockSpec((1024 // steps, 2048), lambda i: (i, 0)),
-            pl.BlockSpec((3, 1024 // steps, 512), lambda i: (0, i, 0)),
-            whole(1, 1024), whole(1, 1024), whole(2, 512), whole(1, 1024),
-            whole(1, 1024), whole(1, 1024), whole(1, 2048), whole(1, 1024),
-        ],
+            rows_in,
+            rows_in,
+            pl.BlockSpec((SIDE, 1024), lambda i: (i, 0)),
+            pl.BlockSpec((SIDE // 4, 1024), lambda i: (i, 0)),
+            pl.BlockSpec((1024, SIDE), lambda i: (0, i)),
+            pl.BlockSpec((3, SIDE // 2, 512), lambda i: (0, i, 0)),
+        ]
+        + [whole(*shape) for shape in vectors],
         out_shape=[
-            jax.ShapeDtypeStruct((4, 512, 1024), f32),
+            jax.ShapeDtypeStruct(lo.shape, bf16),
+            jax.ShapeDtypeStruct(gt.shape, bf16),
+            jax.ShapeDtypeStruct((2048, 1024), f32),
             jax.ShapeDtypeStruct((512, 1024), f32),
             jax.ShapeDtypeStruct((1024, 2048), f32),
             jax.ShapeDtypeStruct((3, 1024, 512), f32),
         ]
-        + [
-            jax.ShapeDtypeStruct(s, f32)
-            for s in ((1, 1024), (1, 1024), (2, 512), (1, 1024), (1, 1024), (1, 1024), (1, 2048), (1, 1024))
-        ],
+        + [jax.ShapeDtypeStruct(shape, f32) for shape in vectors],
         compiler_params=pltpu.CompilerParams(vmem_limit_bytes=56 << 20),
         name="widen",
-    )(a, sum_b, small)
-    down, out, up, qkv, ag, ash, qv, ob, mg, ms, ub, db = got
+    )(sums, sums, sums, sums, small, lo, gt)
+    lo, gt, down, out, up, qkv, ag, ash, qv, ob, mg, ms, ub, db = got
     flat = lambda v: v.reshape(-1)
     return (
-        flat(ag), flat(ash), qkv, qv, out, flat(ob), flat(mg), flat(ms), up, flat(ub),
-        down.reshape(2048, 1024), flat(db),
+        lo, gt, flat(ag), flat(ash), qkv, qv, out, flat(ob), flat(mg), flat(ms), up, flat(ub),
+        down, flat(db),
     )
 
 
@@ -986,15 +1039,14 @@
         row(attn_gain), row(attn_shift), qv_bias, row(out_bias), row(mlp_gain), row(mlp_shift),
         row(up_bias), row(down_bias),
     )
-    layer_output, grad_tokens, sum_a, sum_b, small = layer(
+    layer_output, grad_tokens, sums, small = layer(
         clip_lengths, vectors, tokens, qkv_weight, out_weight, up_weight, down_weight, cotangent
     )
     groups = lax.axis_size("dp")
     if groups > CELL:
         cells = [[k * CELL + i for k in range(groups // CELL)] for i in range(CELL)]
-        wide = (sum_a.astype(f32), sum_b.astype(f32), small)
-        sum_a, sum_b, small = lax.psum(wide, "dp", axis_index_groups=cells)
-    return (layer_output, grad_tokens, *widen(sum_a, sum_b, small))
+        sums, small = lax.psum((sums.astype(f32), small), "dp", axis_index_groups=cells)
+    return widen(sums, small, layer_output, grad_tokens)
 
 
 def solution(mesh):

time: 198 us -> 190 us (0.960)
  Pallas kernels: 195 us -> 189 us
    pallas_call x1, Pallas kernels: 181 us -> 173 us  [layer(): pl.pallas_call(layer_kernel, out_shape=(jax.ShapeDtypeStruct((rows, width...]
where the time goes in v4:
time: 190 us; the launch traced here: 189 us
  Pallas kernels  189 us (99%)
    pallas_call x1, Pallas kernels, layer(): pl.pallas_call(layer_kernel, out_shape=(jax.ShapeDtypeStruct((rows, width...  173 us
    pallas_call x1, Pallas kernels, widen(): pl.pallas_call(widen_kernel, grid=(STEPS,), in_specs=[pl.BlockSpec((4, 1,...  15.8 us

profile of v4, /device:TPU:0, one launch (start us, length us, event | category | flops | bytes accessed | tf_op | source)
XLA Modules:
  0.0 189.4 jit_solution(14471754986058670774)
XLA Ops:
  0.7 172.8 %layer.1 = (bf16[512,1024]{1,0:T(8,128)(2,1)}, bf16[512,1024]{1,0:T(8,128)(2,1)}, bf16[48,2,256,256]{3,2,1,0:T(8,128)(2,1)}, f32[16,1024]{1,0:T(8,128)}) custom-call(s32[1,3]{1,0:T(1,128)} %clip.1, f32[1,1024]{1,0:T(1,128)} %bitcast.15, f32[1,1024]{1,0:T(1,128)} %bitcast.16, f32[2,512]{1,0:T(2,128)} %qvb.1, f32[1,1024]{1,0:T(1,128)} %bitcast.17, ...), custom_call_target="tpu_custom_call" | custom-call | tf_op jit(solution)/shard_map/layer/pallas_call | solution.py:904
  173.4 15.8 %widen.1 = (bf16[512,1024]{1,0:T(8,128)(2,1)}, bf16[512,1024]{1,0:T(8,128)(2,1)}, f32[2048,1024]{1,0:T(8,128)}, f32[512,1024]{1,0:T(8,128)}, f32[1024,2048]{1,0:...) custom-call(bf16[48,2,256,256]{3,2,1,0:T(8,128)(2,1)} %get-tuple-ele, ...), custom_call_target="tpu_custom_call" | custom-call | tf_op jit(solution)/shard_map/widen/pallas_call | solution.py:992

commit v5 on v4

--- a/solution.py
+++ b/solution.py
@@ -8,10 +8,13 @@
 MESH = pl.DeviceIdType.MESH
 bf16, f32 = jnp.bfloat16, jnp.float32
 CELL = 16
-STAGES = 6
+LAGS = (0, 2, 4, 6, 8, 10)
+LAST = LAGS[-1] + 2
+STAGES = len(LAGS)
 SIDE = 256
 N_DOWN = N_UP = 16
 CHUNKS = 24
+END = CHUNKS + LAGS[-1]
 
 
 def pick(low, first, second):
@@ -259,8 +262,8 @@
         self.b_done(i, 6, 6, fin, mine, self.to_sib).wait_recv()
 
     def step(self, t):
-        for stage in (*range(STAGES), STAGES + 1):
-            i = t - stage
+        for stage in range(STAGES + 1):
+            i = t - (*LAGS, LAST)[stage]
 
             def run():
                 if stage < STAGES:
@@ -288,7 +291,7 @@
             self.end_b(i)
             return 0
 
-        lax.fori_loop(CHUNKS - 2, CHUNKS, body, 0)
+        lax.fori_loop(END - LAST, CHUNKS, body, 0)
 
 
 def scratch_of(n, side):
@@ -600,13 +603,13 @@
         row = 6 + piece // 4
         small[pl.ds(row, 1), cols(lax.rem(piece, 4), 256)] = jnp.sum(total, axis=0, keepdims=True)
 
-    def chunk(j, middle=None):
+    def hidden_pair(j):
         hidden(2 * j + 1 - core)
         act_send(j).start()
         pre_send(j).start()
         hidden(2 * j + core)
-        if middle is not None:
-            sm.step(middle)
+
+    def chunk(j):
         mine = cols(2 * j + core, 256)
         act_send(j).wait_recv()
         for n in range(2):
@@ -624,13 +627,12 @@
 
     for i in range(4):
         h2t_send(i).wait_recv()
+    hidden_pair(0)
     chunk(0)
-    sm.step(0)
-    chunk(1, 1)
-    sm.step(2)
-    chunk(2, 3)
-    chunk(3, 4)
-    sm.step(5)
+    for j in range(1, 4):
+        sm.step(j - 1)
+        hidden_pair(j)
+    sm.step(3)
 
     def x_send(name, n, src, dst):
         return rc(name, n, src.at[:, cols(n, 256)], dst.at[:, cols(n, 256)], to_x)
@@ -640,13 +642,18 @@
         x_send("x0", n, xs0, xr0).start()
 
     loop(width // 256, back_two)
-    sm.step(6)
+    chunk(1)
+    sm.step(4)
 
     def forward_two(n):
         xs1[:, cols(n, 256)] = mm(act[...], wdown[:, cols(n, 256)]).astype(bf16)
         x_send("x1", n, xs1, xr1).start()
 
     loop(width // 256, forward_two)
+    sm.step(5)
+    chunk(2)
+    sm.step(6)
+    chunk(3)
     sm.step(7)
 
     for i in range(4):
@@ -666,7 +673,7 @@
 
     total = lax.fori_loop(0, rows // tile, cot_sum, jnp.zeros((8, width), f32), unroll=True)
     small[pl.ds(8, 1), :] = jnp.sum(total, axis=0, keepdims=True)
-    sm.steps(8, 13)
+    sm.steps(8, 10)
 
     for n in range(4):
         x_send("x0", n, xs0, xr0).wait_recv()
@@ -700,8 +707,8 @@
     def back_heads(n):
         dob[:, cols(n, 256)] = mm_nt(dyb[...], wout[t, cols(n, 256), :]).astype(bf16)
 
+    sm.step(10)
     loop(heads_w // 256, back_heads)
-    sm.step(13)
     osib_send(0).wait_recv()
     osib_send(1).wait_recv()
     dyb_out.wait_recv()
@@ -714,7 +721,7 @@
         loc_a[16 + 2 * n] = low[:, :256]
         loc_a[17 + 2 * n] = low[:, 256:]
 
-    sm.step(14)
+    sm.step(11)
 
     def dqkv_send(w, m, src, pr):
         return rc("dqkv", 2 * w + m, src.at[:, cols(pr)], act_sib.at[w, :, cols(m)], to_sib)
@@ -747,12 +754,13 @@
             dqkv_send(w, m, src, pr).start()
 
     loop(2, theirs)
-    sm.step(15)
+    sm.step(12)
 
     def ours(m):
         attend_back(2 * core + m)
 
     loop(2, ours)
+    sm.step(13)
     h1t_out.wait_recv()
     for w, src in enumerate((q, k, v)):
         for m in range(2):
@@ -765,7 +773,7 @@
                 loc_a[20 + at] = low.astype(bf16)
             else:
                 loc_b[12 + at] = low.astype(bf16)
-    sm.step(16)
+    sm.step(14)
 
     last = wup.at[pl.ds(0, rows), pl.ds(0, width)]
 
@@ -777,7 +785,7 @@
         x_send("x2", n, xs0, last).start()
 
     loop(width // 256, back_one)
-    sm.steps(17, 20)
+    sm.steps(15, 18)
 
     for n in range(4):
         x_send("x1", n, xs1, xr1).wait_recv()
@@ -792,7 +800,7 @@
     lo_out = load(6, hid, lo_h)
     lo_out.start()
 
-    sm.steps(20, 23)
+    sm.steps(18, 20)
     for n in range(4):
         x_send("x2", n, xs0, last).wait_recv()
     sums[...] = jnp.zeros_like(sums)
@@ -824,11 +832,11 @@
     small_mid = small_rc(3, small_r.at[2], sm.to_mid)
     small_out = small_rc(4, small_r.at[3], sm.to_z)
     small_sib.start()
-    sm.step(23)
+    sm.step(20)
     small_sib.wait_recv()
     small_r[0] += small[...]
     small_y.start()
-    sm.step(24)
+    sm.step(21)
     small_y.wait_recv()
     small_r[1] += small_r[0]
 
@@ -836,7 +844,7 @@
     def _():
         small_in.start()
 
-    sm.step(25)
+    sm.step(22)
 
     @pl.when(sm.mid)
     def _():
@@ -844,7 +852,7 @@
         small_r[2] += small_r[1]
         small_mid.start()
 
-    sm.step(26)
+    sm.step(23)
 
     @pl.when(sm.mid)
     def _():
@@ -852,7 +860,7 @@
         small_r[3] += small_r[2]
         small_out.start()
 
-    sm.steps(27, CHUNKS + STAGES - 1)
+    sm.steps(24, END)
 
     @pl.when(sm.outer)
     def _():

time: 190 us -> 187 us (0.984)
  Pallas kernels: 189 us -> 185 us
    pallas_call x1, Pallas kernels: 173 us -> 170 us  [layer(): pl.pallas_call(layer_kernel, out_shape=(jax.ShapeDtypeStruct((rows, width...]
where the time goes in v5:
time: 187 us; the launch traced here: 186 us
  Pallas kernels  185 us (99%)
    pallas_call x1, Pallas kernels, layer(): pl.pallas_call(layer_kernel, out_shape=(jax.ShapeDtypeStruct((rows, width...  170 us
    pallas_call x1, Pallas kernels, widen(): pl.pallas_call(widen_kernel, grid=(STEPS,), in_specs=[pl.BlockSpec((4, 1,...  15.8 us

profile of v5, /device:TPU:0, one launch (start us, length us, event | category | flops | bytes accessed | tf_op | source)
XLA Modules:
  0.0 186.2 jit_solution(6943143810864285367)
XLA Ops:
  0.7 169.6 %layer.1 = (bf16[512,1024]{1,0:T(8,128)(2,1)}, bf16[512,1024]{1,0:T(8,128)(2,1)}, bf16[48,2,256,256]{3,2,1,0:T(8,128)(2,1)}, f32[16,1024]{1,0:T(8,128)}) custom-call(s32[1,3]{1,0:T(1,128)} %clip.1, f32[1,1024]{1,0:T(1,128)} %bitcast.15, f32[1,1024]{1,0:T(1,128)} %bitcast.16, f32[2,512]{1,0:T(2,128)} %qvb.1, f32[1,1024]{1,0:T(1,128)} %bitcast.17, ...), custom_call_target="tpu_custom_call" | custom-call | tf_op jit(solution)/shard_map/layer/pallas_call | solution.py:912
  170.3 15.8 %widen.1 = (bf16[512,1024]{1,0:T(8,128)(2,1)}, bf16[512,1024]{1,0:T(8,128)(2,1)}, f32[2048,1024]{1,0:T(8,128)}, f32[512,1024]{1,0:T(8,128)}, f32[1024,2048]{1,0:...) custom-call(bf16[48,2,256,256]{3,2,1,0:T(8,128)(2,1)} %get-tuple-ele, ...), custom_call_target="tpu_custom_call" | custom-call | tf_op jit(solution)/shard_map/widen/pallas_call | solution.py:1000

commit v6 on v5

--- a/solution.py
+++ b/solution.py
@@ -800,7 +800,7 @@
     lo_out = load(6, hid, lo_h)
     lo_out.start()
 
-    sm.steps(18, 20)
+    sm.steps(18, 27)
     for n in range(4):
         x_send("x2", n, xs0, last).wait_recv()
     sums[...] = jnp.zeros_like(sums)
@@ -832,11 +832,11 @@
     small_mid = small_rc(3, small_r.at[2], sm.to_mid)
     small_out = small_rc(4, small_r.at[3], sm.to_z)
     small_sib.start()
-    sm.step(20)
+    sm.step(27)
     small_sib.wait_recv()
     small_r[0] += small[...]
     small_y.start()
-    sm.step(21)
+    sm.step(28)
     small_y.wait_recv()
     small_r[1] += small_r[0]
 
@@ -844,7 +844,7 @@
     def _():
         small_in.start()
 
-    sm.step(22)
+    sm.step(29)
 
     @pl.when(sm.mid)
     def _():
@@ -852,7 +852,7 @@
         small_r[2] += small_r[1]
         small_mid.start()
 
-    sm.step(23)
+    sm.step(30)
 
     @pl.when(sm.mid)
     def _():
@@ -860,7 +860,7 @@
         small_r[3] += small_r[2]
         small_out.start()
 
-    sm.steps(24, END)
+    sm.steps(31, END)
 
     @pl.when(sm.outer)
     def _():

time: 187 us -> 186 us (level)
  no operation moved by 1% of the time
where the time goes in v6:
time: 186 us
  Pallas kernels  185 us (99%)
    pallas_call x1, Pallas kernels, layer(): pl.pallas_call(layer_kernel, out_shape=(jax.ShapeDtypeStruct((rows, width...  169 us
    pallas_call x1, Pallas kernels, widen(): pl.pallas_call(widen_kernel, grid=(STEPS,), in_specs=[pl.BlockSpec((4, 1,...  15.8 us

profile of v6, /device:TPU:0, one launch (start us, length us, event | category | flops | bytes accessed | tf_op | source)
XLA Modules:
  0.0 185.6 jit_solution(3050379897447484064)
XLA Ops:
  0.7 168.9 %layer.1 = (bf16[512,1024]{1,0:T(8,128)(2,1)}, bf16[512,1024]{1,0:T(8,128)(2,1)}, bf16[48,2,256,256]{3,2,1,0:T(8,128)(2,1)}, f32[16,1024]{1,0:T(8,128)}) custom-call(s32[1,3]{1,0:T(1,128)} %clip.1, f32[1,1024]{1,0:T(1,128)} %bitcast.15, f32[1,1024]{1,0:T(1,128)} %bitcast.16, f32[2,512]{1,0:T(2,128)} %qvb.1, f32[1,1024]{1,0:T(1,128)} %bitcast.17, ...), custom_call_target="tpu_custom_call" | custom-call | tf_op jit(solution)/shard_map/layer/pallas_call | solution.py:912
  169.6 15.8 %widen.1 = (bf16[512,1024]{1,0:T(8,128)(2,1)}, bf16[512,1024]{1,0:T(8,128)(2,1)}, f32[2048,1024]{1,0:T(8,128)}, f32[512,1024]{1,0:T(8,128)}, f32[1024,2048]{1,0:...) custom-call(bf16[48,2,256,256]{3,2,1,0:T(8,128)(2,1)} %get-tuple-ele, ...), custom_call_target="tpu_custom_call" | custom-call | tf_op jit(solution)/shard_map/widen/pallas_call | solution.py:1000

commit v7 on v6

--- a/solution.py
+++ b/solution.py
@@ -638,18 +638,20 @@
         return rc(name, n, src.at[:, cols(n, 256)], dst.at[:, cols(n, 256)], to_x)
 
     def back_two(n):
-        xs0[:, cols(n, 256)] = mm_nt(pre[...], wup[cols(n, 256), :]).astype(bf16)
-        x_send("x0", n, xs0, xr0).start()
-
-    loop(width // 256, back_two)
+        xs0[:, cols(n, 512)] = mm_nt(pre[...], wup[cols(n, 512), :]).astype(bf16)
+        x_send("x0", 2 * n, xs0, xr0).start()
+        x_send("x0", 2 * n + 1, xs0, xr0).start()
+
+    loop(width // 512, back_two)
     chunk(1)
     sm.step(4)
 
     def forward_two(n):
-        xs1[:, cols(n, 256)] = mm(act[...], wdown[:, cols(n, 256)]).astype(bf16)
-        x_send("x1", n, xs1, xr1).start()
-
-    loop(width // 256, forward_two)
+        xs1[:, cols(n, 512)] = mm(act[...], wdown[:, cols(n, 512)]).astype(bf16)
+        x_send("x1", 2 * n, xs1, xr1).start()
+        x_send("x1", 2 * n + 1, xs1, xr1).start()
+
+    loop(width // 512, forward_two)
     sm.step(5)
     chunk(2)
     sm.step(6)
@@ -678,7 +680,7 @@
     for n in range(4):
         x_send("x0", n, xs0, xr0).wait_recv()
     sums[...] = jnp.zeros_like(sums)
-    back = 128
+    back = 256
     dyb = xr0
 
     def norm_two_back(i):

time: 186 us -> 190 us (1.022); the launches traced: 186 us -> 186 us
  no operation moved by 1% of the time
where the time goes in v7:
time: 190 us; the launch traced here: 186 us
  Pallas kernels  185 us (97%)
    pallas_call x1, Pallas kernels, layer(): pl.pallas_call(layer_kernel, out_shape=(jax.ShapeDtypeStruct((rows, width...  169 us
    pallas_call x1, Pallas kernels, widen(): pl.pallas_call(widen_kernel, grid=(STEPS,), in_specs=[pl.BlockSpec((4, 1,...  15.8 us

profile of v7, /device:TPU:0, one launch (start us, length us, event | category | flops | bytes accessed | tf_op | source)
XLA Modules:
  0.0 185.8 jit_solution(18414147403364656563)
XLA Ops:
  0.7 168.9 %layer.1 = (bf16[512,1024]{1,0:T(8,128)(2,1)}, bf16[512,1024]{1,0:T(8,128)(2,1)}, bf16[48,2,256,256]{3,2,1,0:T(8,128)(2,1)}, f32[16,1024]{1,0:T(8,128)}) custom-call(s32[1,3]{1,0:T(1,128)} %clip.1, f32[1,1024]{1,0:T(1,128)} %bitcast.15, f32[1,1024]{1,0:T(1,128)} %bitcast.16, f32[2,512]{1,0:T(2,128)} %qvb.1, f32[1,1024]{1,0:T(1,128)} %bitcast.17, ...), custom_call_target="tpu_custom_call" | custom-call | tf_op jit(solution)/shard_map/layer/pallas_call | solution.py:914
  169.6 15.8 %widen.1 = (bf16[512,1024]{1,0:T(8,128)(2,1)}, bf16[512,1024]{1,0:T(8,128)(2,1)}, f32[2048,1024]{1,0:T(8,128)}, f32[512,1024]{1,0:T(8,128)}, f32[1024,2048]{1,0:...) custom-call(bf16[48,2,256,256]{3,2,1,0:T(8,128)(2,1)} %get-tuple-ele, ...), custom_call_target="tpu_custom_call" | custom-call | tf_op jit(solution)/shard_map/widen/pallas_call | solution.py:1002
